TPU v7x, 512 devices: a whole 4x8x8 slice. The times are simulated.
512 devices in a mesh: frame: 8 (over x, core), row: 32 (over z_lo, y), head: 2 (over z_hi).
Axes of the slice: x: 4, y: 8, z: 8 (z_hi: 2, z_lo: 4; z = z_hi * 4 + z_lo), core: 2. Of those that a mesh axis runs over, the one named last changes fastest.
Arguments:
- q_pre: bfloat16 [8, 64, 64, 2560], P('frame', 'row', None, 'head'), may hold values from -60 to 60
- k_pre: bfloat16 [8, 64, 64, 2560], P('frame', 'row', None, 'head'), may hold values from -60 to 60
- values: bfloat16 [8, 64, 64, 2560], P('frame', 'row', None, 'head'), may hold values from -6 to 6
- target: bfloat16 [8, 64, 64, 2560], P('frame', 'row', None, 'head'), may hold values from -6 to 6
- gain_q: float32 [2560], P('head'), may hold values from 0.5 to 2
- gain_k: float32 [2560], P('head'), may hold values from 0.5 to 2
- kept: int32 [8, 64, 4], replicated, may hold values 0 or 1
Outputs:
- grad_q: bfloat16 [8, 64, 64, 2560], P('frame', 'row', None, 'head')
- grad_k: bfloat16 [8, 64, 64, 2560], P('frame', 'row', None, 'head')
- grad_v: bfloat16 [8, 64, 64, 2560], P('frame', 'row', None, 'head')
All inputs are finite; a program needn't handle non-finite values.
Results may differ from a plain program's by a relative error of at most 0.0107.
The roundings to bfloat16 on the way count: a program that leaves them out, or rounds other values in their place, can miss the bound.
Values may be sent and summed in bfloat16 or wider, within the bound.
A program may use at most 128 MiB of HBM per device.

v0:
```python
import jax
import jax.numpy as jnp
from jax import lax
from jax.sharding import PartitionSpec as P

TC = 16
HEADS = 20
HD = 128


norm_eps = 1e-06


def padded(x, sides, width):
    for axis, dim in sides:
        size, length = (lax.axis_size(axis), x.shape[dim])
        up = [(i, (i + 1) % size) for i in range(size - 1)]
        down = [(j, i) for i, j in up]
        last = lax.slice_in_dim(x, length - width, length, axis=dim)
        first = lax.slice_in_dim(x, 0, width, axis=dim)
        before = lax.ppermute(last, axis, up)
        after = lax.ppermute(first, axis, down)
        x = jnp.concatenate([before, x, after], axis=dim)
    return x


def from_behind(value, axis, steps):
    count = lax.axis_size(axis)
    first, last = (max(0, -steps), min(count, count - steps))
    return lax.ppermute(value, axis, [(source, source + steps) for source in range(first, last)])


def query_mask(kept_win, col_tile, tiles):
    near_cols = jnp.abs(col_tile[:, None] - col_tile[None, :]) <= 1
    same_tile = col_tile[:, None] == col_tile[None, :]
    one_hot = col_tile[:, None] == jnp.arange(tiles)[None, :]
    key_kept = jnp.any(one_hot[None, None] & (kept_win[:, :, None, :] > 0), axis=-1)
    centre = (jnp.arange(3)[:, None] == 1) & (jnp.arange(3)[None, :] == 1)
    allowed = near_cols[:, None, None, :] & (
        key_kept[None] | centre[None, :, :, None] & same_tile[:, None, None, :]
    )
    return allowed.reshape(col_tile.shape[0], -1)


def attend_line(query, kv_win, t_line, allowed):
    width, heads_dev, _ = query.shape
    score_scale = HD ** (-0.5)
    key_block = kv_win[0].reshape(9 * width, heads_dev, HD)
    value_block = kv_win[1].reshape(9 * width, heads_dev, HD)
    mask = allowed[None]
    scores = (
        jnp.einsum("qhd,khd->hqk", query, key_block, preferred_element_type=jnp.float32)
        * score_scale
    )
    scores = jnp.where(mask, scores, -jnp.inf)
    row_max = jnp.max(scores, -1, keepdims=True)
    expo = jnp.where(mask, jnp.exp(scores - row_max), 0.0)
    denominator = jnp.sum(expo, -1, keepdims=True)
    probability = expo / denominator
    prob_b = probability.astype(jnp.bfloat16)
    attended = jnp.einsum("hqk,khd->qhd", prob_b, value_block, preferred_element_type=jnp.float32)
    d_out = (attended - t_line.astype(jnp.float32)).astype(jnp.bfloat16)
    delta_sum = jnp.sum(d_out.astype(jnp.float32) * attended, -1).T
    prob_grad = jnp.einsum("qhd,khd->hqk", d_out, value_block, preferred_element_type=jnp.float32)
    score_grad = (probability * (prob_grad - delta_sum[:, :, None]) * score_scale).astype(
        jnp.bfloat16
    )
    dq_line = jnp.einsum("hqk,khd->qhd", score_grad, key_block, preferred_element_type=jnp.float32)
    log_total = row_max[..., 0] + jnp.log(denominator[..., 0])
    return (dq_line.reshape(width, heads_dev * HD), d_out, log_total, delta_sum, prob_b, score_grad)


def per_device(q_pre, k_pre, values, target, gain_q, gain_k, kept):
    frames, rows, width, feat_dev = q_pre.shape
    heads_dev = feat_dev // HD
    tiles = width // TC
    features = HEADS * HD
    line_count = frames * rows
    col_tile = jnp.arange(width) // TC
    q_float = q_pre.astype(jnp.float32)
    k_float = k_pre.astype(jnp.float32)
    square_q, square_k = lax.psum(
        (jnp.sum(q_float * q_float, -1), jnp.sum(k_float * k_float, -1)), "head"
    )
    scale_q = lax.rsqrt(square_q[..., None] / features + norm_eps)
    scale_k = lax.rsqrt(square_k[..., None] / features + norm_eps)
    q_norm = (q_float * scale_q * gain_q).astype(jnp.bfloat16)
    k_norm = (k_float * scale_k * gain_k).astype(jnp.bfloat16)
    kv_ext = padded(jnp.stack([k_norm, values]), (("frame", 1), ("row", 2)), 1)
    frame_at = lax.axis_index("frame")
    row_at = lax.axis_index("row")
    zero = jnp.int32(0)
    kept_pad = jnp.pad(kept, ((1, 1), (1, 1), (0, 0)))
    kept_ext = lax.dynamic_slice(
        kept_pad, (frame_at * frames, row_at * rows, zero), (frames + 2, rows + 2, tiles)
    )
    line_ids = jnp.arange(line_count, dtype=jnp.int32)
    q_lines = q_norm.reshape(line_count, width, heads_dev, HD)
    t_lines = target.reshape(line_count, width, heads_dev, HD)

    def query_window(line):
        f_at = line // rows
        r_at = line % rows
        kv_win = lax.dynamic_slice(
            kv_ext, (zero, f_at, r_at, zero, zero), (2, 3, 3, width, feat_dev)
        )
        kept_win = lax.dynamic_slice(kept_ext, (f_at, r_at, zero), (3, 3, tiles))
        return (f_at, r_at, kv_win, query_mask(kept_win, col_tile, tiles))

    def returned_step(totals, inputs):
        line, query, t_line = inputs
        f_at, r_at, kv_win, allowed = query_window(line)
        dq_line, d_out, log_total, delta_sum, prob_b, score_grad = attend_line(
            query, kv_win, t_line, allowed
        )
        key_grad = jnp.einsum("hqk,qhd->khd", score_grad, query, preferred_element_type=jnp.float32)
        value_grad = jnp.einsum("hqk,qhd->khd", prob_b, d_out, preferred_element_type=jnp.float32)
        both = jnp.stack(
            [key_grad.reshape(3, 3, width, feat_dev), value_grad.reshape(3, 3, width, feat_dev)]
        )
        start = (zero, f_at, r_at, zero, zero)
        current = lax.dynamic_slice(totals, start, (2, 3, 3, width, feat_dev))
        totals = lax.dynamic_update_slice(totals, current + both, start)
        return (totals, dq_line)

    empty = jnp.zeros((2, frames + 2, rows + 2, width, feat_dev), jnp.float32)
    totals, dq_lines = lax.scan(returned_step, empty, (line_ids, q_lines, t_lines))
    inner = totals[:, :, 1 : rows + 1]
    row_edges = (totals[:, :, 0:1], totals[:, :, rows + 1 : rows + 2])
    row_moved = [
        from_behind(row_edges[side], "row", by_value) for side, by_value in ((0, -1), (1, 1))
    ]
    inner = inner.at[:, :, rows - 1 : rows].add(row_moved[0])
    inner = inner.at[:, :, 0:1].add(row_moved[1])
    middle = inner[:, 1 : frames + 1]
    frame_edges = (inner[:, 0:1], inner[:, frames + 1 : frames + 2])
    frame_moved = [
        from_behind(frame_edges[side], "frame", by_value) for side, by_value in ((0, -1), (1, 1))
    ]
    middle = middle.at[:, frames - 1 : frames].add(frame_moved[0])
    middle = middle.at[:, 0:1].add(frame_moved[1])
    dk_norm = middle[0]
    value_total = middle[1]
    dq_norm = dq_lines.reshape(frames, rows, width, feat_dev)
    gated_q = gain_q * dq_norm
    gated_k = gain_k * dk_norm
    sum_q, sum_k = lax.psum(
        (jnp.sum(q_float * gated_q, -1), jnp.sum(k_float * gated_k, -1)), "head"
    )
    grad_q = (scale_q * gated_q - q_float * scale_q**3 * sum_q[..., None] / features).astype(
        jnp.bfloat16
    )
    grad_k = (scale_k * gated_k - k_float * scale_k**3 * sum_k[..., None] / features).astype(
        jnp.bfloat16
    )
    return (grad_q, grad_k, value_total.astype(jnp.bfloat16))


def solution(mesh):
    return jax.shard_map(
        per_device,
        mesh=mesh,
        in_specs=(
            P("frame", "row", None, "head"),
            P("frame", "row", None, "head"),
            P("frame", "row", None, "head"),
            P("frame", "row", None, "head"),
            P("head"),
            P("head"),
            P(),
        ),
        out_specs=(
            P("frame", "row", None, "head"),
            P("frame", "row", None, "head"),
            P("frame", "row", None, "head"),
        ),
        check_vma=False,
    )
```

profile of v0, /device:TPU:66, one launch (start us, length us, event | category | flops | bytes accessed | tf_op | source)
XLA Modules:
  0.0 290.2 jit_solution(1067938665325009301)
XLA Ops:
  0.6 1.2 fusion.36
  1.8 1.1 fusion.44
  2.9 11.0 %all-reduce.2 = (f32[1,2,64]{2,1,0:T(2,128)S(1)}, f32[1,2,64]{2,1,0:T(2,128)S(1)}) all-reduce(f32[1,2,64]{2,1,0:T(2,128)S(1)} %bitcast.101, f32[1,2,64]{2,1,0:T(2,128)S(1)} %bitcast.102), channel_id=1, replica_groups=mesh['frame'=8,'row'=32,'head'=2] {'head'}, use_global_device_ids=true, to_apply=%region_1.2 | all-reduce | flops 256 | bytes 2048 | tf_op jit(solution)/shard_map/psum | solution.py:82
  14.0 1.1 fusion.54
  15.1 1.0 pad_maximum_fusion.2
  16.1 1.9 collective-permute-start.1
  18.1 2.4 collective-permute-start
  20.5 5.7 %collective-permute-done.1 = bf16[2,1,2,64,1280]{4,3,2,1,0:T(8,128)(2,1)S(1)} collective-permute-done((bf16[2,1,2,64,1280]{4,3,2,1,0:T(8,128)(2,1)S(1)}, bf16[2,1,2,64,1280]{4,3,2,1,0:T(8,128)(2,1)S(1)}, u32[]{:S(2)}, u32[]{:S(2)}) %collective-permute-start.1) | collective-permute-done | bytes 655392 | tf_op jit(solution)/shard_map/ppermute | solution.py:22
  26.2 3.8 %collective-permute-done = bf16[2,1,2,64,1280]{4,3,2,1,0:T(8,128)(2,1)S(1)} collective-permute-done((bf16[2,1,2,64,1280]{4,3,2,1,0:T(8,128)(2,1)S(1)}, bf16[2,1,2,64,1280]{4,3,2,1,0:T(8,128)(2,1)S(1)}, u32[]{:S(2)}, u32[]{:S(2)}) %collective-permute-start) | collective-permute-done | bytes 655392 | tf_op jit(solution)/shard_map/ppermute | solution.py:21
  30.2 1.4 fusion.63
  31.6 3.5 %collective-permute-start.2 = (bf16[2,3,1,64,1280]{4,3,2,1,0:T(8,128)(2,1)}, bf16[2,3,1,64,1280]{4,3,2,1,0:T(8,128)(2,1)}, u32[]{:S(2)}, u32[]{:S(2)}) collective-permute-start(bf16[2,3,1,64,1280]{4,3,2,1,0:T(8,128)(2,1)} %get-tuple-element.287), channel_id=1, source_target_pairs={{0,2},{2,4},{4,6},{6,8},{8,10},{10,12},{12,14},{14,16},{16,18},{18... | collective-permute-start | bytes 2949128 | tf_op jit(solution)/shard_map/ppermute | solution.py:21
  35.1 4.5 %collective-permute-start.3 = (bf16[2,3,1,64,1280]{4,3,2,1,0:T(8,128)(2,1)}, bf16[2,3,1,64,1280]{4,3,2,1,0:T(8,128)(2,1)}, u32[]{:S(2)}, u32[]{:S(2)}) collective-permute-start(bf16[2,3,1,64,1280]{4,3,2,1,0:T(8,128)(2,1)} %get-tuple-element.288), channel_id=1, source_target_pairs={{2,0},{4,2},{6,4},{8,6},{10,8},{12,10},{14,12},{16,14},{18,16},{20... | collective-permute-start | bytes 2949128 | tf_op jit(solution)/shard_map/ppermute | solution.py:22
  40.3 1.2 reshape.461
  41.4 0.8 copy.33
  42.3 16.4 %collective-permute-done.2 = bf16[2,3,1,64,1280]{4,3,2,1,0:T(8,128)(2,1)} collective-permute-done((bf16[2,3,1,64,1280]{4,3,2,1,0:T(8,128)(2,1)}, bf16[2,3,1,64,1280]{4,3,2,1,0:T(8,128)(2,1)}, u32[]{:S(2)}, u32[]{:S(2)}) %collective-permute-start.2) | collective-permute-done | bytes 983072 | tf_op jit(solution)/shard_map/ppermute | solution.py:21
  58.7 1.2 collective-permute-done.3
  59.9 3.3 %pad_maximum_fusion = bf16[2,3,4,64,1280]{4,3,2,1,0:T(8,128)(2,1)} fusion(bf16[2,3,1,64,1280]{4,3,2,1,0:T(8,128)(2,1)} %collective-permute-done.3, bf16[2,1,2,64,1280]{4,3,2,1,0:T(8,128)(2,1)S(1)} %collective-permute-done.1, bf16[1,1,2,64,1280]{4,3,2,1,0:T(8,128)(2,1)S(1)} %bitcast.100, bf16[1,1,2,64,1280]{4,3,2,1,0:T(8,128)(2,1)S(1)} %fusion.54, ...), kind=kLoop, calls=%fused_computation.48 | loop fusion | flops 9830400 | bytes 7864320 | tf_op jit(solution)/shard_map/concatenate | solution.py:23
  63.2 3.9 %broadcast_in_dim.66 = f32[2,3,4,64,1280]{4,3,2,1,0:T(8,128)} broadcast(f32[]{:T(128)} %constant.235.clone.1), dimensions={} | broadcast | bytes 7864324 | tf_op jit(solution)/shard_map/broadcast_in_dim | solution.py:126
  67.2 93.6 %while.22 = (s32[]{:T(128)}, f32[2,3,4,64,1280]{4,3,2,1,0:T(8,128)}, f32[2,64,1280]{2,1,0:T(8,128)}, s32[2]{0:T(128)S(1)}, bf16[2,64,10,128]{3,1,2,0:T(8,128)(2,...) while((s32[]{:T(128)}, ...), condition=%wide.region_9.10_spmd.clone.clone, body=%wide.region_4.9_spmd.clone.clone.sunk | while | flops 574964416 | bytes 103695864 | solution.py:127
  67.2 0.6 dynamic_slice.85
  70.4 2.0 constant_dynamic-slice_fusion.3
  72.4 2.5 squeeze.45
  74.9 2.4 squeeze.46
  77.3 4.2 %fusion.92 = (f32[10,64]{1,0:T(8,128)S(1)}, f32[10,64,576]{2,1,0:T(8,128)}) fusion(bf16[576,10,128]{2,1,0:T(8,128)(2,1)} %squeeze.46, pred[64,576]{1,0:T(8,128)(4,1)S(1)} %copy.62, bf16[2,64,10,128]{3,1,2,0:T(8,128)(2,1)S(1)} %get-tuple-element.388, s32[]{:T(128)S(6)} %copy.71), kind=kOutput, calls=%fused_computation.90.clone.1 | convolution fusion | flops 96215616 | bytes 3197444 | tf_op jit(solution)/shard_map/while/body/eval_jaxpr/sub | solution.py:57
  81.5 2.5 multiply_reduce_fusion.2
  84.0 1.0 multiply_convert_fusion.2
  85.0 0.7 copy-done.1
  85.7 0.7 convolution_bitcast_fusion.9
  87.1 2.6 convolution_bitcast_fusion.7
  89.7 3.9 %copy.63 = f32[576,10,128]{2,1,0:T(8,128)} copy(f32[576,10,128]{2,0,1:T(8,128)S(1)} %convolution_bitcast_fusion.7) | data formatting | bytes 5898240 | tf_op jit(solution)/shard_map/while/body/eval_jaxpr/hqk,qhd->khd/transpose | solution.py:117
  93.6 3.2 %reshape.472 = f32[1,3,3,64,1280]{4,3,2,1,0:T(8,128)S(1)} reshape(f32[576,10,128]{2,1,0:T(8,128)} %copy.63) | data formatting | bytes 5898240 | tf_op jit(solution)/shard_map/while/body/eval_jaxpr/stack;while/body/eval_jaxpr/reshape | solution.py:118
  96.8 1.8 convolution_bitcast_fusion.8
  98.6 3.9 %copy.64 = f32[576,10,128]{2,1,0:T(8,128)} copy(f32[576,10,128]{2,0,1:T(8,128)S(1)} %convolution_bitcast_fusion.8) | data formatting | bytes 5898240 | tf_op jit(solution)/shard_map/while/body/eval_jaxpr/hqk,qhd->khd/transpose | solution.py:116
  102.5 4.7 %reshape.473 = f32[1,3,3,64,1280]{4,3,2,1,0:T(8,128)} reshape(f32[576,10,128]{2,1,0:T(8,128)} %copy.64) | data formatting | bytes 5898240 | tf_op jit(solution)/shard_map/while/body/eval_jaxpr/stack;while/body/eval_jaxpr/reshape | solution.py:118
  107.1 6.8 %fusion.93 = f32[2,3,4,64,1280]{4,3,2,1,0:T(8,128)} fusion(f32[2,3,4,64,1280]{4,3,2,1,0:T(8,128)} %get-tuple-element.372, s32[]{:T(128)S(6)} %select_n.86, f32[1,3,3,64,1280]{4,3,2,1,0:T(8,128)S(1)} %reshape.472, f32[1,3,3,64,1280]{4,3,2,1,0:T(8,128)} %reshape.473), kind=kLoop, calls=%fused_computation.3.clone.1 | loop fusion | flops 2949120 | bytes 17694724 | tf_op jit(solution)/shard_map/while/body/eval_jaxpr/dynamic_update_slice | solution.py:123
  117.2 2.0 constant_dynamic-slice_fusion.3
  119.2 2.5 squeeze.45
  121.7 2.4 squeeze.46
  124.1 4.2 %fusion.92 = (f32[10,64]{1,0:T(8,128)S(1)}, f32[10,64,576]{2,1,0:T(8,128)}) fusion(bf16[576,10,128]{2,1,0:T(8,128)(2,1)} %squeeze.46, pred[64,576]{1,0:T(8,128)(4,1)S(1)} %copy.62, bf16[2,64,10,128]{3,1,2,0:T(8,128)(2,1)S(1)} %get-tuple-element.388, s32[]{:T(128)S(6)} %copy.71), kind=kOutput, calls=%fused_computation.90.clone.1 | convolution fusion | flops 96215616 | bytes 3197444 | tf_op jit(solution)/shard_map/while/body/eval_jaxpr/sub | solution.py:57
  128.3 2.5 multiply_reduce_fusion.2
  130.8 1.0 multiply_convert_fusion.2
  131.8 0.6 copy-done.1
  132.5 0.7 convolution_bitcast_fusion.9
  133.9 2.6 convolution_bitcast_fusion.7
  136.5 3.9 %copy.63 = f32[576,10,128]{2,1,0:T(8,128)} copy(f32[576,10,128]{2,0,1:T(8,128)S(1)} %convolution_bitcast_fusion.7) | data formatting | bytes 5898240 | tf_op jit(solution)/shard_map/while/body/eval_jaxpr/hqk,qhd->khd/transpose | solution.py:117
  140.4 3.2 %reshape.472 = f32[1,3,3,64,1280]{4,3,2,1,0:T(8,128)S(1)} reshape(f32[576,10,128]{2,1,0:T(8,128)} %copy.63) | data formatting | bytes 5898240 | tf_op jit(solution)/shard_map/while/body/eval_jaxpr/stack;while/body/eval_jaxpr/reshape | solution.py:118
  143.6 1.8 convolution_bitcast_fusion.8
  145.4 3.9 %copy.64 = f32[576,10,128]{2,1,0:T(8,128)} copy(f32[576,10,128]{2,0,1:T(8,128)S(1)} %convolution_bitcast_fusion.8) | data formatting | bytes 5898240 | tf_op jit(solution)/shard_map/while/body/eval_jaxpr/hqk,qhd->khd/transpose | solution.py:116
  149.3 4.7 %reshape.473 = f32[1,3,3,64,1280]{4,3,2,1,0:T(8,128)} reshape(f32[576,10,128]{2,1,0:T(8,128)} %copy.64) | data formatting | bytes 5898240 | tf_op jit(solution)/shard_map/while/body/eval_jaxpr/stack;while/body/eval_jaxpr/reshape | solution.py:118
  154.0 6.8 %fusion.93 = f32[2,3,4,64,1280]{4,3,2,1,0:T(8,128)} fusion(f32[2,3,4,64,1280]{4,3,2,1,0:T(8,128)} %get-tuple-element.372, s32[]{:T(128)S(6)} %select_n.86, f32[1,3,3,64,1280]{4,3,2,1,0:T(8,128)S(1)} %reshape.472, f32[1,3,3,64,1280]{4,3,2,1,0:T(8,128)} %reshape.473), kind=kLoop, calls=%fused_computation.3.clone.1 | loop fusion | flops 2949120 | bytes 17694724 | tf_op jit(solution)/shard_map/while/body/eval_jaxpr/dynamic_update_slice | solution.py:123
  160.7 1.7 slice.174
  162.4 7.0 %collective-permute-start.4 = (f32[2,3,1,64,1280]{4,3,2,1,0:T(8,128)S(1)}, f32[2,3,1,64,1280]{4,3,2,1,0:T(8,128)S(1)}, u32[]{:S(2)}, u32[]{:S(2)}) collective-permute-start(f32[2,3,1,64,1280]{4,3,2,1,0:T(8,128)S(1)} %slice.174), channel_id=1, source_target_pairs={{2,0},{4,2},{6,4},{8,6},{10,8},{12,10},{14,12},{16,14},{18,16},{20... | collective-permute-start | bytes 5898248 | tf_op jit(solution)/shard_map/ppermute | solution.py:30
  169.4 2.4 slice.172
  171.8 37.6 %collective-permute-done.4 = f32[2,3,1,64,1280]{4,3,2,1,0:T(8,128)S(1)} collective-permute-done((f32[2,3,1,64,1280]{4,3,2,1,0:T(8,128)S(1)}, f32[2,3,1,64,1280]{4,3,2,1,0:T(8,128)S(1)}, u32[]{:S(2)}, u32[]{:S(2)}) %collective-permute-start.4) | collective-permute-done | bytes 1966112 | tf_op jit(solution)/shard_map/ppermute | solution.py:30
  209.8 2.6 collective-permute-start.5
  212.4 44.0 %collective-permute-done.5 = f32[2,3,1,64,1280]{4,3,2,1,0:T(8,128)S(1)} collective-permute-done((f32[2,3,1,64,1280]{4,3,2,1,0:T(8,128)S(1)}, f32[2,3,1,64,1280]{4,3,2,1,0:T(8,128)S(1)}, u32[]{:S(2)}, u32[]{:S(2)}) %collective-permute-start.5) | collective-permute-done | bytes 1966112 | tf_op jit(solution)/shard_map/ppermute | solution.py:30
  257.1 2.1 collective-permute-start.6
  259.2 2.4 collective-permute-start.7
  261.8 12.4 %collective-permute-done.6 = f32[2,1,2,64,1280]{4,3,2,1,0:T(8,128)S(1)} collective-permute-done((f32[2,1,2,64,1280]{4,3,2,1,0:T(8,128)S(1)}, f32[2,1,2,64,1280]{4,3,2,1,0:T(8,128)S(1)}, u32[]{:S(2)}, u32[]{:S(2)}) %collective-permute-start.6) | collective-permute-done | bytes 1310752 | tf_op jit(solution)/shard_map/ppermute | solution.py:30
  274.3 3.8 %collective-permute-done.7 = f32[2,1,2,64,1280]{4,3,2,1,0:T(8,128)S(1)} collective-permute-done((f32[2,1,2,64,1280]{4,3,2,1,0:T(8,128)S(1)}, f32[2,1,2,64,1280]{4,3,2,1,0:T(8,128)S(1)}, u32[]{:S(2)}, u32[]{:S(2)}) %collective-permute-start.7) | collective-permute-done | bytes 1310752 | tf_op jit(solution)/shard_map/ppermute | solution.py:30
  278.6 0.8 fusion.53
  279.3 8.8 %all-reduce.1 = (f32[2,64]{1,0:T(2,128)S(1)}, f32[2,64]{1,0:T(2,128)S(1)}) all-reduce(f32[2,64]{1,0:T(2,128)S(1)} %fusion.43, f32[2,64]{1,0:T(2,128)S(1)} %fusion.51), channel_id=1, replica_groups=mesh['frame'=8,'row'=32,'head'=2] {'head'}, use_global_device_ids=true, to_apply=%region_11.12 | all-reduce | flops 256 | bytes 2048 | tf_op jit(solution)/shard_map/psum | solution.py:147
  288.1 1.0 fusion.42
  289.2 1.0 fusion.50
  (109 shorter events, 6.3 us)
Async XLA Ops:
  0.6 29.4 %copy-start.7 = (bf16[1,2,64,1280]{3,2,1,0:T(8,128)(2,1)S(1)}, bf16[1,2,64,1280]{3,2,1,0:T(8,128)(2,1)}, u32[]{:S(2)}) copy-start(bf16[1,2,64,1280]{3,2,1,0:T(8,128)(2,1)} %param.23) | copy-start | bytes 983044
  13.9 16.0 %copy-start.20 = (f32[1,2,64]{2,1,0:T(2,128)}, f32[1,2,64]{2,1,0:T(2,128)S(1)}, u32[]{:S(2)}) copy-start(f32[1,2,64]{2,1,0:T(2,128)S(1)} %get-tuple-element.273) | copy-start | bytes 1540
  13.9 16.0 %copy-start.22 = (f32[1,2,64]{2,1,0:T(2,128)}, f32[1,2,64]{2,1,0:T(2,128)S(1)}, u32[]{:S(2)}) copy-start(f32[1,2,64]{2,1,0:T(2,128)S(1)} %get-tuple-element.274) | copy-start | bytes 1540
  13.9 1.1 copy-start.16
  14.0 25.8 %copy-start.18 = (f32[2,64]{1,0:T(2,128)}, f32[2,64]{1,0:T(2,128)S(1)}, u32[]{:S(2)}) copy-start(f32[2,64]{1,0:T(2,128)S(1)} %get-tuple-element.292) | copy-start | bytes 1540
  16.1 10.0 %collective-permute-start.1 = (bf16[2,1,2,64,1280]{4,3,2,1,0:T(8,128)(2,1)S(1)}, bf16[2,1,2,64,1280]{4,3,2,1,0:T(8,128)(2,1)S(1)}, u32[]{:S(2)}, u32[]{:S(2)}) collective-permute-start(bf16[2,1,2,64,1280]{4,3,2,1,0:T(8,128)(2,1)S(1)} %pad_maximum_fusion.2), channel_id=1, source_target_pairs={{64,0},{128,64},{192,128},{256,192},{320,256},{384,320},{448,384},... | collective-permute-start | bytes 1966088 | tf_op jit(solution)/shard_map/ppermute | solution.py:22
  18.1 11.9 %collective-permute-start = (bf16[2,1,2,64,1280]{4,3,2,1,0:T(8,128)(2,1)S(1)}, bf16[2,1,2,64,1280]{4,3,2,1,0:T(8,128)(2,1)S(1)}, u32[]{:S(2)}, u32[]{:S(2)}) collective-permute-start(bf16[2,1,2,64,1280]{4,3,2,1,0:T(8,128)(2,1)S(1)} %pad_maximum_fusion.2), channel_id=1, source_target_pairs={{0,64},{64,128},{128,192},{192,256},{256,320},{320,384},{384,448},... | collective-permute-start | bytes 1966088 | tf_op jit(solution)/shard_map/ppermute | solution.py:21
  30.2 9.4 %copy-start.15 = (s32[8,64,4]{1,2,0:T(4,128)S(1)}, s32[8,64,4]{1,2,0:T(4,128)}, u32[]{:S(2)}) copy-start(s32[8,64,4]{1,2,0:T(4,128)} %param.27) | copy-start | bytes 24580
  30.2 9.6 %copy-start.4 = (bf16[1,2,64,1280]{3,2,1,0:T(8,128)(2,1)S(1)}, bf16[1,2,64,1280]{3,2,1,0:T(8,128)(2,1)}, u32[]{:S(2)}) copy-start(bf16[1,2,64,1280]{3,2,1,0:T(8,128)(2,1)} %param.21) | copy-start | bytes 983044
  30.2 9.6 %copy-start.12 = (f32[1280]{0:T(1024)S(1)}, f32[1280]{0:T(1024)}, u32[]{:S(2)}) copy-start(f32[1280]{0:T(1024)} %param.25) | copy-start | bytes 15364
  31.6 27.1 %collective-permute-start.2 = (bf16[2,3,1,64,1280]{4,3,2,1,0:T(8,128)(2,1)}, bf16[2,3,1,64,1280]{4,3,2,1,0:T(8,128)(2,1)}, u32[]{:S(2)}, u32[]{:S(2)}) collective-permute-start(bf16[2,3,1,64,1280]{4,3,2,1,0:T(8,128)(2,1)} %get-tuple-element.287), channel_id=1, source_target_pairs={{0,2},{2,4},{4,6},{6,8},{8,10},{10,12},{12,14},{14,16},{16,18},{18... | collective-permute-start | bytes 2949128 | tf_op jit(solution)/shard_map/ppermute | solution.py:21
  35.1 24.8 %collective-permute-start.3 = (bf16[2,3,1,64,1280]{4,3,2,1,0:T(8,128)(2,1)}, bf16[2,3,1,64,1280]{4,3,2,1,0:T(8,128)(2,1)}, u32[]{:S(2)}, u32[]{:S(2)}) collective-permute-start(bf16[2,3,1,64,1280]{4,3,2,1,0:T(8,128)(2,1)} %get-tuple-element.288), channel_id=1, source_target_pairs={{2,0},{4,2},{6,4},{8,6},{10,8},{12,10},{14,12},{16,14},{18,16},{20... | collective-permute-start | bytes 2949128 | tf_op jit(solution)/shard_map/ppermute | solution.py:22
  77.3 4.2 %copy-start.2 = (bf16[576,10,128]{2,1,0:T(8,128)(2,1)S(1)}, bf16[576,10,128]{2,1,0:T(8,128)(2,1)}, u32[]{:S(2)}) copy-start(bf16[576,10,128]{2,1,0:T(8,128)(2,1)} %squeeze.45) | copy-start | bytes 4423684 | tf_op jit(solution)/shard_map/while
  77.3 4.2 %copy-start.11 = (bf16[2,64,10,128]{3,1,2,0:T(8,128)(2,1)S(1)}, bf16[2,64,10,128]{3,1,2,0:T(8,128)(2,1)}, u32[]{:S(2)}) copy-start(bf16[2,64,10,128]{3,1,2,0:T(8,128)(2,1)} %get-tuple-element.391) | copy-start | bytes 983044 | tf_op jit(solution)/shard_map/while
  81.5 2.5 copy-start.24
  84.0 1.7 copy-start.1
  85.7 0.9 copy-start.3
  85.7 1.4 copy-start.8
  87.1 2.6 copy-start.9
  124.1 4.2 %copy-start.2 = (bf16[576,10,128]{2,1,0:T(8,128)(2,1)S(1)}, bf16[576,10,128]{2,1,0:T(8,128)(2,1)}, u32[]{:S(2)}) copy-start(bf16[576,10,128]{2,1,0:T(8,128)(2,1)} %squeeze.45) | copy-start | bytes 4423684 | tf_op jit(solution)/shard_map/while
  124.1 4.2 %copy-start.11 = (bf16[2,64,10,128]{3,1,2,0:T(8,128)(2,1)S(1)}, bf16[2,64,10,128]{3,1,2,0:T(8,128)(2,1)}, u32[]{:S(2)}) copy-start(bf16[2,64,10,128]{3,1,2,0:T(8,128)(2,1)} %get-tuple-element.391) | copy-start | bytes 983044 | tf_op jit(solution)/shard_map/while
  128.3 2.5 copy-start.24
  130.8 1.7 copy-start.1
  132.5 0.9 copy-start.3
  132.5 1.4 copy-start.8
  133.9 2.6 copy-start.9
  162.4 47.0 %copy-start = (f32[2,3,4,64,1280]{4,3,2,1,0:T(8,128)S(1)}, f32[2,3,4,64,1280]{4,3,2,1,0:T(8,128)}, u32[]{:S(2)}) copy-start(f32[2,3,4,64,1280]{4,3,2,1,0:T(8,128)} %get-tuple-element.189) | copy-start | bytes 23592964
  162.4 47.0 %collective-permute-start.4 = (f32[2,3,1,64,1280]{4,3,2,1,0:T(8,128)S(1)}, f32[2,3,1,64,1280]{4,3,2,1,0:T(8,128)S(1)}, u32[]{:S(2)}, u32[]{:S(2)}) collective-permute-start(f32[2,3,1,64,1280]{4,3,2,1,0:T(8,128)S(1)} %slice.174), channel_id=1, source_target_pairs={{2,0},{4,2},{6,4},{8,6},{10,8},{12,10},{14,12},{16,14},{18,16},{20... | collective-permute-start | bytes 5898248 | tf_op jit(solution)/shard_map/ppermute | solution.py:30
  209.8 46.6 %collective-permute-start.5 = (f32[2,3,1,64,1280]{4,3,2,1,0:T(8,128)S(1)}, f32[2,3,1,64,1280]{4,3,2,1,0:T(8,128)S(1)}, u32[]{:S(2)}, u32[]{:S(2)}) collective-permute-start(f32[2,3,1,64,1280]{4,3,2,1,0:T(8,128)S(1)} %get-tuple-element.283), channel_id=1, source_target_pairs={{0,2},{2,4},{4,6},{6,8},{8,10},{10,12},{12,14},{14,16},{16,18},{18... | collective-permute-start | bytes 5898248 | tf_op jit(solution)/shard_map/ppermute | solution.py:30
  256.8 4.7 %copy-start.21 = (f32[1,2,64]{2,1,0:T(2,128)S(1)}, f32[1,2,64]{2,1,0:T(2,128)}, u32[]{:S(2)}) copy-start(f32[1,2,64]{2,1,0:T(2,128)} %copy-done.20) | copy-start | bytes 1540
  256.9 4.7 %copy-start.23 = (f32[1,2,64]{2,1,0:T(2,128)S(1)}, f32[1,2,64]{2,1,0:T(2,128)}, u32[]{:S(2)}) copy-start(f32[1,2,64]{2,1,0:T(2,128)} %copy-done.22) | copy-start | bytes 1540
  256.9 4.7 %copy-start.5 = (bf16[1,2,64,1280]{3,2,1,0:T(8,128)(2,1)S(1)}, bf16[1,2,64,1280]{3,2,1,0:T(8,128)(2,1)}, u32[]{:S(2)}) copy-start(bf16[1,2,64,1280]{3,2,1,0:T(8,128)(2,1)} %param.21) | copy-start | bytes 983044
  256.9 4.7 %copy-start.10 = (f32[2,64,1280]{2,1,0:T(8,128)S(1)}, f32[2,64,1280]{2,1,0:T(8,128)}, u32[]{:S(2)}) copy-start(f32[2,64,1280]{2,1,0:T(8,128)} %get-tuple-element.188) | copy-start | bytes 1966084
  256.9 4.7 %copy-start.13 = (f32[1280]{0:T(1024)S(1)}, f32[1280]{0:T(1024)}, u32[]{:S(2)}) copy-start(f32[1280]{0:T(1024)} %param.25) | copy-start | bytes 15364
  257.1 17.2 %collective-permute-start.6 = (f32[2,1,2,64,1280]{4,3,2,1,0:T(8,128)S(1)}, f32[2,1,2,64,1280]{4,3,2,1,0:T(8,128)S(1)}, u32[]{:S(2)}, u32[]{:S(2)}) collective-permute-start(f32[2,1,2,64,1280]{4,3,2,1,0:T(8,128)S(1)} %get-tuple-element.285), channel_id=1, source_target_pairs={{64,0},{128,64},{192,128},{256,192},{320,256},{384,320},{448,384},... | collective-permute-start | bytes 3932168 | tf_op jit(solution)/shard_map/ppermute | solution.py:30
  259.2 18.9 %collective-permute-start.7 = (f32[2,1,2,64,1280]{4,3,2,1,0:T(8,128)S(1)}, f32[2,1,2,64,1280]{4,3,2,1,0:T(8,128)S(1)}, u32[]{:S(2)}, u32[]{:S(2)}) collective-permute-start(f32[2,1,2,64,1280]{4,3,2,1,0:T(8,128)S(1)} %get-tuple-element.286), channel_id=1, source_target_pairs={{0,64},{64,128},{128,192},{192,256},{256,320},{320,384},{384,448},... | collective-permute-start | bytes 3932168 | tf_op jit(solution)/shard_map/ppermute | solution.py:30
  261.8 16.5 %copy-start.6 = (bf16[1,2,64,1280]{3,2,1,0:T(8,128)(2,1)S(1)}, bf16[1,2,64,1280]{3,2,1,0:T(8,128)(2,1)}, u32[]{:S(2)}) copy-start(bf16[1,2,64,1280]{3,2,1,0:T(8,128)(2,1)} %param.22) | copy-start | bytes 983044
  261.8 16.5 %copy-start.14 = (f32[1280]{0:T(1024)S(1)}, f32[1280]{0:T(1024)}, u32[]{:S(2)}) copy-start(f32[1280]{0:T(1024)} %param.26) | copy-start | bytes 15364
  261.8 26.3 %copy-start.19 = (f32[2,64]{1,0:T(2,128)S(1)}, f32[2,64]{1,0:T(2,128)}, u32[]{:S(2)}) copy-start(f32[2,64]{1,0:T(2,128)} %copy-done.18) | copy-start | bytes 1540
  278.4 10.8 %copy-start.17 = (f32[2,64]{1,0:T(2,128)S(1)}, f32[2,64]{1,0:T(2,128)}, u32[]{:S(2)}) copy-start(f32[2,64]{1,0:T(2,128)} %copy-done.16) | copy-start | bytes 1540
where the time goes:
time: 291 us; the launch traced here: 290 us
  waiting for transfers between devices  125 us (43%)
  local copies, waits for them, and re-layouts  62.6 us (22%)
  starting transfers between devices  26.3 us (9%)
  other arithmetic  26.2 us (9%)
  matrix products  25.6 us (9%)
  blocking collectives  19.8 us (7%)
  loops' own time  3.7 us (1%)
    ppermute x4, waiting for transfers between devices, from_behind(): lax.ppermute(value, axis, [(source, source + steps) for source in range(f...  97.9 us
    ppermute x2, waiting for transfers between devices, padded(): before = lax.ppermute(last, axis, up)  20.3 us
    reshape x4, local copies, waits for them, and re-layouts, returned_step(): jnp.stack([key_grad.reshape(3, 3, width, feat_dev), value_grad.reshape(3,...  15.7 us
    ppermute x4, starting transfers between devices, from_behind(): lax.ppermute(value, axis, [(source, source + steps) for source in range(f...  14 us
    dynamic_update_slice x2, other arithmetic, returned_step(): totals = lax.dynamic_update_slice(totals, current + both, start)  13.6 us
    psum x1, blocking collectives, per_device(): lax.psum((jnp.sum(q_float * q_float, -1), jnp.sum(k_float * k_float, -1))...  11 us
    psum x1, blocking collectives, per_device(): lax.psum((jnp.sum(q_float * gated_q, -1), jnp.sum(k_float * gated_k, -1))...  8.82 us
    sub x2, matrix products, attend_line(): expo = jnp.where(mask, jnp.exp(scores - row_max), 0.0)  8.45 us
  transfers between devices with their start and end apart: 8, of which 8 were waited for; matrix products, arithmetic and copies ran while one was open for 2% of the time, Pallas kernels for 0%

commit v1 on v0

v1 whole, which is shorter than its diff:
```python
import functools

import jax
import jax.numpy as jnp
from jax import lax
from jax.experimental import pallas as pl
from jax.experimental.pallas import tpu as pltpu
from jax.sharding import PartitionSpec as P

TC = 16
HD = 128
TILES = 4
MESH = pl.DeviceIdType.MESH
norm_eps = 1e-06
LOG2E = 1.4426950408889634
SCORE_SCALE = HD ** (-0.5)
NEG = -1e30

BF16 = jnp.bfloat16
F32 = jnp.float32
ROWS_T = (((0,), (0,)), ((), ()))
COLS_T = (((1,), (1,)), ((), ()))
PLAIN = (((1,), (0,)), ((), ()))


def dot(a, b, dims):
    return lax.dot_general(a, b, dims, preferred_element_type=F32)


def columns_to_rows(col_a, col_b):
    lane = lax.broadcasted_iota(jnp.int32, (128, 128), 1)
    both = jnp.where(lane < 4, jnp.broadcast_to(col_a, (128, 128)), jnp.broadcast_to(col_b, (128, 128)))
    return both.T[0:8]


def rows_to_columns(rows):
    sub = lax.broadcasted_iota(jnp.int32, (128, 128), 0)
    both = jnp.where(
        sub < 64,
        jnp.broadcast_to(rows[0:1], (128, 128)),
        jnp.broadcast_to(rows[4:5], (128, 128)),
    ).T
    return both[:, 0:1], both[:, 64:65]


def kernel(
    sizes, features, q_ref, k_ref, v_ref, t_ref, gq_ref, gk_ref, kept_ref,
    oq_ref, ok_ref, ov_ref,
    kv, qn, bias, gx_out, gx_in, gy_out, gy_in, own, dq, acc, hx_out, hx_in,
    row_s, row_r, fr_s, fr_r, co_s, co_r, gx_s, gx_r, gy_s, gy_r, hx_s, hx_r,
):
    frames, rows, heads = sizes
    chunks, _, _, _, width, wide = kv.shape
    per = wide // HD
    tokens = 2 * width
    f_at, r_at, h_at = (lax.axis_index(a) for a in ("frame", "row", "head"))
    frame_id = [(f_at - 1, r_at, h_at), (f_at + 1, r_at, h_at)]
    row_id = [(f_at, r_at - 1, h_at), (f_at, r_at + 1, h_at)]
    head_id = (f_at, r_at, 1 - h_at)
    has_f = [f_at > 0, f_at < frames - 1]
    has_r = [r_at > 0, r_at < rows - 1]

    barrier = pltpu.get_barrier_semaphore()
    pl.semaphore_signal(barrier, inc=1, device_id=head_id, device_id_type=MESH)
    for s in (0, 1):
        for has, ids in ((has_f, frame_id), (has_r, row_id)):

            @pl.when(has[s])
            def _():
                pl.semaphore_signal(barrier, inc=1, device_id=ids[s], device_id_type=MESH)

    def remote(src, dst, send, recv, device):
        return pltpu.make_async_remote_copy(
            src_ref=src, dst_ref=dst, send_sem=send, recv_sem=recv,
            device_id=device, device_id_type=MESH,
        )

    def row_out(c, a, s):
        return remote(kv.at[c, a, 1, 1 + s], kv.at[c, a, 1, 3 - 3 * s],
                      row_s.at[c, a, s], row_r.at[c, a, 1 - s], row_id[s])

    def row_in(c, a, s):
        return remote(kv.at[c, a, 1, 1 + s], kv.at[c, a, 1, 3 * s],
                      row_s.at[c, a, s], row_r.at[c, a, s], row_id[s])

    def frame_out(c, a, s):
        return remote(kv.at[c, a, 1, pl.ds(1, 2)], kv.at[c, a, 2 - 2 * s, pl.ds(1, 2)],
                      fr_s.at[c, a, s], fr_r.at[c, a, 1 - s], frame_id[s])

    def frame_in(c, a, s):
        return remote(kv.at[c, a, 1, pl.ds(1, 2)], kv.at[c, a, 2 * s, pl.ds(1, 2)],
                      fr_s.at[c, a, s], fr_r.at[c, a, s], frame_id[s])

    def corner_out(c, a, s, t):
        return remote(kv.at[c, a, 1, 3 * t], kv.at[c, a, 2 - 2 * s, 3 * t],
                      co_s.at[c, a, s, t], co_r.at[c, a, 1 - s, t], frame_id[s])

    def corner_in(c, a, s, t):
        return remote(kv.at[c, a, 1, 3 * t], kv.at[c, a, 2 * s, 3 * t],
                      co_s.at[c, a, s, t], co_r.at[c, a, s, t], frame_id[s])

    def gx_copy(c, s, mine):
        return remote(gx_out.at[c, s], gx_in.at[c, s if mine else 1 - s],
                      gx_s.at[c, s], gx_r.at[c, s if mine else 1 - s], frame_id[s])

    def gy_copy(c, s, mine):
        return remote(gy_out.at[c, s], gy_in.at[c, s if mine else 1 - s],
                      gy_s.at[c, s], gy_r.at[c, s if mine else 1 - s], row_id[s])

    def hx_copy(i):
        return remote(hx_out.at[i], hx_in.at[i], hx_s.at[i], hx_r.at[i], head_id)

    def lanes(c):
        return slice(c * wide, (c + 1) * wide)

    for c in range(chunks):
        kv[c, 1, 1, 1:3] = v_ref[0, :, :, lanes(c)]
    for s in (0, 1):

        @pl.when(jnp.logical_not(has_f[s]))
        def _():
            def body(c, carry):
                kv[c, :, 2 * s] = jnp.zeros((2, 4, width, wide), BF16)
                gx_in[c, s] = jnp.zeros((2, 4, width, wide), BF16)
                return carry

            lax.fori_loop(0, chunks, body, 0)

        @pl.when(jnp.logical_not(has_r[s]))
        def _():
            def body(c, carry):
                for a in (0, 1):
                    for d in range(3):
                        kv[c, a, d, 3 * s] = jnp.zeros((width, wide), BF16)
                gy_in[c, s] = jnp.zeros((2, width, wide), BF16)
                return carry

            lax.fori_loop(0, chunks, body, 0)

    square_q = jnp.zeros((tokens, 128), F32)
    square_k = jnp.zeros((tokens, 128), F32)
    for i in range(chunks * per):
        part = slice(i * HD, (i + 1) * HD)
        q_part = q_ref[0, :, :, part].reshape(tokens, HD).astype(F32)
        k_part = k_ref[0, :, :, part].reshape(tokens, HD).astype(F32)
        square_q += q_part * q_part
        square_k += k_part * k_part
    hx_out[0] = columns_to_rows(
        jnp.sum(square_q, -1, keepdims=True), jnp.sum(square_k, -1, keepdims=True)
    )

    peers = 1
    for edge in (*has_f, *has_r):
        peers = peers + edge.astype(jnp.int32)
    pl.semaphore_wait(barrier, peers)

    hx_copy(0).start()

    def send_own(c, a):
        for s in (0, 1):

            @pl.when(has_r[s])
            def _():
                row_out(c, a, s).start()

            @pl.when(has_f[s])
            def _():
                frame_out(c, a, s).start()

    def v_body(c, carry):
        send_own(c, 1)
        return carry

    lax.fori_loop(0, chunks, v_body, 0)

    keys = 12 * width
    key = lax.broadcasted_iota(jnp.int32, (1, keys), 1)
    key_line = key // TC
    kept_row = jnp.zeros((1, keys), jnp.int32)
    for d in range(3):
        frame = f_at + (d - 1)
        frame_ok = jnp.logical_and(frame >= 0, frame < frames)
        for g in range(4):
            row = 2 * r_at + (g - 1)
            ok = jnp.logical_and(frame_ok, jnp.logical_and(row >= 0, row < 2 * rows))
            for tile in range(TILES):
                one = kept_ref[jnp.clip(frame, 0, frames - 1), jnp.clip(row, 0, 2 * rows - 1), tile]
                one = jnp.where(ok, one, 0)
                kept_row = jnp.where(key_line == (d * 4 + g) * TILES + tile, one, kept_row)
    query = lax.broadcasted_iota(jnp.int32, (tokens, keys), 0)
    keyb = lax.broadcasted_iota(jnp.int32, (tokens, keys), 1)
    q_row, q_tile = query // width + 1, (query % width) // TC
    k_line, k_tile = keyb // width, (keyb % width) // TC
    k_row = k_line % 4
    near = (jnp.abs(q_row - k_row) <= 1) & (jnp.abs(q_tile - k_tile) <= 1)
    same = (k_line == q_row + 4) & (q_tile == k_tile)
    kept_full = jnp.broadcast_to(kept_row, (tokens, keys)) > 0
    bias[...] = jnp.where(near & (kept_full | same), 0.0, NEG)

    hx_copy(0).wait()
    scale_q, scale_k = rows_to_columns(
        lax.rsqrt((hx_out[0] + hx_in[0]) / features + norm_eps)
    )
    for c in range(chunks):
        k_norm = k_ref[0, :, :, lanes(c)].reshape(tokens, wide).astype(F32) * scale_k
        k_norm = (k_norm * gk_ref[:, lanes(c)]).astype(BF16)
        kv[c, 0, 1, 1:3] = k_norm.reshape(2, width, wide)
        send_own(c, 0)
    for c in range(chunks):
        q_norm = q_ref[0, :, :, lanes(c)].reshape(tokens, wide).astype(F32) * scale_q
        qn[c] = (q_norm * gq_ref[:, lanes(c)]).astype(BF16)

    for a in (1, 0):

        def relay(c, carry, a=a):
            for t in (0, 1):

                @pl.when(has_r[t])
                def _():
                    row_in(c, a, t).wait_recv()

                for s in (0, 1):

                    @pl.when(jnp.logical_and(has_r[t], has_f[s]))
                    def _():
                        corner_out(c, a, s, t).start()

            return carry

        lax.fori_loop(0, chunks, relay, 0)

    acc[...] = jnp.zeros_like(acc)

    def finish_x(c):
        for s in (0, 1):

            @pl.when(has_f[s])
            def _():
                gx_copy(c, s, True).wait_recv()

        for a in (0, 1):
            for g in range(4):
                total = own[c, a, g] + gx_in[c, 0, a, g].astype(F32) + gx_in[c, 1, a, g].astype(F32)
                if g in (0, 3):
                    gy_out[c, g // 3, a] = total.astype(BF16)
                else:
                    own[c, a, g] = total
        for s in (0, 1):

            @pl.when(has_r[s])
            def _():
                gy_copy(c, s, False).start()

    def compute(c, carry):
        for s in (0, 1):

            @pl.when(has_f[s])
            def _():
                for a in (0, 1):
                    frame_in(c, a, s).wait_recv()

            for t in (0, 1):

                @pl.when(jnp.logical_and(has_r[t], has_f[s]))
                def _():
                    for a in (0, 1):
                        corner_in(c, a, s, t).wait_recv()

        for j in range(per):
            part = slice(j * HD, (j + 1) * HD)
            at = pl.ds(pl.multiple_of(c * wide + j * HD, HD), HD)
            query_h = qn[c, :, part]
            key_h = kv[c, 0, :, :, :, part].reshape(keys, HD)
            value_h = kv[c, 1, :, :, :, part].reshape(keys, HD)
            scores = dot(query_h, key_h, COLS_T) * (SCORE_SCALE * LOG2E) + bias[...]
            expo = jnp.exp2(scores - jnp.max(scores, -1, keepdims=True))
            prob = expo * (1.0 / jnp.sum(expo, -1, keepdims=True))
            prob_b = prob.astype(BF16)
            attended = dot(prob_b, value_h, PLAIN)
            target = t_ref[0, :, :, at].reshape(tokens, HD).astype(F32)
            d_out = (attended - target).astype(BF16)
            delta = jnp.sum(d_out.astype(F32) * attended, -1, keepdims=True)
            prob_grad = dot(d_out, value_h, COLS_T)
            score_grad = (prob * ((prob_grad - delta) * SCORE_SCALE)).astype(BF16)
            dq_h = dot(score_grad, key_h, PLAIN)
            gated = dq_h * gq_ref[:, at]
            dq[c, :, part] = gated
            acc[0] += gated * q_ref[0, :, :, at].reshape(tokens, HD).astype(F32)
            for a, grad in (
                (0, dot(score_grad, query_h, ROWS_T)),
                (1, dot(prob_b, d_out, ROWS_T)),
            ):
                grad = grad.reshape(3, 4, width, HD)
                own[c, a, :, :, part] = grad[1]
                for s in (0, 1):
                    gx_out[c, s, a, :, :, part] = grad[2 * s].astype(BF16)
        for s in (0, 1):

            @pl.when(has_f[s])
            def _():
                gx_copy(c, s, False).start()

        @pl.when(c >= 2)
        def _():
            finish_x(c - 2)

        return carry

    lax.fori_loop(0, chunks, compute, 0)

    def last_x(c, carry):
        finish_x(c)
        return carry

    lax.fori_loop(max(chunks - 2, 0), chunks, last_x, 0)

    def finish_y(c, carry):
        at = pl.ds(pl.multiple_of(c * wide, HD), wide)
        for s in (0, 1):

            @pl.when(has_r[s])
            def _():
                gy_copy(c, s, True).wait_recv()

        ov_ref[0, :, :, at] = (own[c, 1, 1:3] + gy_in[c, :, 1].astype(F32)).astype(BF16)
        gated = (own[c, 0, 1:3] + gy_in[c, :, 0].astype(F32)).reshape(tokens, wide) * gk_ref[:, at]
        own[c, 0, 1:3] = gated.reshape(2, width, wide)
        product = gated * k_ref[0, :, :, at].reshape(tokens, wide).astype(F32)
        for j in range(per):
            acc[1] += product[:, j * HD : (j + 1) * HD]
        return carry

    lax.fori_loop(0, chunks, finish_y, 0)

    hx_out[1] = columns_to_rows(
        jnp.sum(acc[0], -1, keepdims=True), jnp.sum(acc[1], -1, keepdims=True)
    )
    hx_copy(1).start()
    hx_copy(1).wait()
    sum_q, sum_k = rows_to_columns((hx_out[1] + hx_in[1]) / features)
    back_q = scale_q * scale_q * scale_q * sum_q
    back_k = scale_k * scale_k * scale_k * sum_k
    for c in range(chunks):
        q_float = q_ref[0, :, :, lanes(c)].reshape(tokens, wide).astype(F32)
        grad_q = scale_q * dq[c] - q_float * back_q
        oq_ref[0, :, :, lanes(c)] = grad_q.astype(BF16).reshape(2, width, wide)
        k_float = k_ref[0, :, :, lanes(c)].reshape(tokens, wide).astype(F32)
        grad_k = scale_k * own[c, 0, 1:3].reshape(tokens, wide) - k_float * back_k
        ok_ref[0, :, :, lanes(c)] = grad_k.astype(BF16).reshape(2, width, wide)

    def drain(c, carry):
        for s in (0, 1):

            @pl.when(has_r[s])
            def _():
                for a in (0, 1):
                    row_out(c, a, s).wait_send()
                gy_copy(c, s, False).wait_send()

            @pl.when(has_f[s])
            def _():
                for a in (0, 1):
                    frame_out(c, a, s).wait_send()
                gx_copy(c, s, False).wait_send()

            for t in (0, 1):

                @pl.when(jnp.logical_and(has_r[t], has_f[s]))
                def _():
                    for a in (0, 1):
                        corner_out(c, a, s, t).wait_send()

        return carry

    lax.fori_loop(0, chunks, drain, 0)


def per_device(sizes, per, q_pre, k_pre, values, target, gain_q, gain_k, kept):
    _, _, width, feat_dev = q_pre.shape
    chunks, wide = feat_dev // (per * HD), per * HD
    dma = pltpu.SemaphoreType.DMA
    vmem = pl.BlockSpec(memory_space=pltpu.VMEM)
    out = jax.ShapeDtypeStruct(q_pre.shape, BF16)
    return pl.pallas_call(
        functools.partial(kernel, sizes, feat_dev * sizes[2]),
        out_shape=(out, out, out),
        in_specs=[vmem] * 6 + [pl.BlockSpec(memory_space=pltpu.SMEM)],
        out_specs=(vmem, vmem, vmem),
        scratch_shapes=[
            pltpu.VMEM((chunks, 2, 3, 4, width, wide), BF16),
            pltpu.VMEM((chunks, 2 * width, wide), BF16),
            pltpu.VMEM((2 * width, 12 * width), F32),
            pltpu.VMEM((chunks, 2, 2, 4, width, wide), BF16),
            pltpu.VMEM((chunks, 2, 2, 4, width, wide), BF16),
            pltpu.VMEM((chunks, 2, 2, width, wide), BF16),
            pltpu.VMEM((chunks, 2, 2, width, wide), BF16),
            pltpu.VMEM((chunks, 2, 4, width, wide), F32),
            pltpu.VMEM((chunks, 2 * width, wide), F32),
            pltpu.VMEM((2, 2 * width, HD), F32),
            pltpu.VMEM((2, 8, 128), F32),
            pltpu.VMEM((2, 8, 128), F32),
            dma((chunks, 2, 2)),
            dma((chunks, 2, 2)),
            dma((chunks, 2, 2)),
            dma((chunks, 2, 2)),
            dma((chunks, 2, 2, 2)),
            dma((chunks, 2, 2, 2)),
            dma((chunks, 2)),
            dma((chunks, 2)),
            dma((chunks, 2)),
            dma((chunks, 2)),
            dma((2,)),
            dma((2,)),
        ],
        compiler_params=pltpu.CompilerParams(collective_id=0, has_side_effects=True),
    )(q_pre, k_pre, values, target, gain_q[None], gain_k[None], kept)


def solution(mesh):
    sizes = tuple(mesh.shape[a] for a in ("frame", "row", "head"))
    grid = P("frame", "row", None, "head")
    return jax.shard_map(
        functools.partial(per_device, sizes, 2),
        mesh=mesh,
        in_specs=(grid, grid, grid, grid, P("head"), P("head"), P()),
        out_specs=(grid, grid, grid),
        check_vma=False,
    )
```

time: 291 us -> 68.8 us (0.24)
  the two profiles are of different devices: /device:TPU:66 before, /device:TPU:30 now
where the time goes in v1:
time: 68.8 us; the launch traced here: 68.5 us
  Pallas kernels  60.8 us (88%)
  local copies, waits for them, and re-layouts  7.04 us (10%)
    pallas_call x1, Pallas kernels, per_device(): pl.pallas_call(functools.partial(kernel, sizes, feat_dev * sizes[2]), out...  60.8 us
    unnamed x10, local copies, waits for them, and re-layouts  4.45 us

profile of v1, /device:TPU:30, one launch (start us, length us, event | category | flops | bytes accessed | tf_op | source)
XLA Modules:
  0.0 68.5 jit_solution(17048950050220720407)
XLA Ops:
  0.6 0.0 copy-start.2
  0.6 1.3 %broadcast_in_dim.6.gq_ref = f32[1,1280]{1,0:T(1,128)} reshape(f32[1280]{0:T(1024)} %param.11) | data formatting | bytes 10240 | tf_op jit(solution)/shard_map/broadcast_in_dim | solution.py:416
  1.9 1.3 %broadcast_in_dim.7.gk_ref = f32[1,1280]{1,0:T(1,128)} reshape(f32[1280]{0:T(1024)} %param.12) | data formatting | bytes 10240 | tf_op jit(solution)/shard_map/broadcast_in_dim | solution.py:416
  3.2 0.0 copy-done.2
  3.2 0.9 %copy.10.kept_ref = s32[8,64,4]{2,1,0:T(8,128)} copy(s32[8,64,4]{1,2,0:T(4,128)S(1)} %copy-done.2) | data formatting | bytes 16384 | tf_op args[6]
  4.1 60.8 %shard_map.94 = (bf16[1,2,64,1280]{3,2,1,0:T(8,128)(2,1)}, bf16[1,2,64,1280]{3,2,1,0:T(8,128)(2,1)}, bf16[1,2,64,1280]{3,2,1,0:T(8,128)(2,1)}) custom-call(bf16[1,2,64,1280]{3,2,1,0:T(8,128)(2,1)} %q_ref.1, bf16[1,2,64,1280]{3,2,1,0:T(8,128)(2,1)} %k_ref.1, bf16[1,2,64,1280]{3,2,1,0:T(8,128)(2,1)} %v_ref.1, bf16[1,2,64,1280]{3,2,1,0:T(8,128)(2,1)} %t_ref.1, ...), custom_call_target="tpu_custom_call" | custom-call | tf_op jit(solution)/shard_map/pallas_call | solution.py:384
  64.9 0.0 copy-start.1
  64.9 1.8 %copy.14 = bf16[1,2,64,1280]{3,2,1,0:T(8,128)(2,1)} copy(bf16[1,2,64,1280]{3,2,1,0:T(8,128)(2,1)} %get-tuple-element.6) | data formatting | bytes 655360
  66.7 0.0 copy-done.1
  66.7 0.0 copy-start
  66.7 0.7 %copy.15 = bf16[1,2,64,1280]{3,2,1,0:T(8,128)(2,1)} copy(bf16[1,2,64,1280]{3,2,1,0:T(8,128)(2,1)S(1)} %copy-done.1) | data formatting | bytes 655360
  67.4 0.4 copy-done
  67.8 0.7 %copy.16 = bf16[1,2,64,1280]{3,2,1,0:T(8,128)(2,1)} copy(bf16[1,2,64,1280]{3,2,1,0:T(8,128)(2,1)S(1)} %copy-done) | data formatting | bytes 655360
Async XLA Ops:
  0.6 2.6 %copy-start.2 = (s32[8,64,4]{1,2,0:T(4,128)S(1)}, s32[8,64,4]{1,2,0:T(4,128)}, u32[]{:S(2)}) copy-start(s32[8,64,4]{1,2,0:T(4,128)} %param.13) | copy-start | bytes 24580
  64.9 1.8 %copy-start.1 = (bf16[1,2,64,1280]{3,2,1,0:T(8,128)(2,1)S(1)}, bf16[1,2,64,1280]{3,2,1,0:T(8,128)(2,1)}, u32[]{:S(2)}) copy-start(bf16[1,2,64,1280]{3,2,1,0:T(8,128)(2,1)} %get-tuple-element.7) | copy-start | bytes 983044
  66.7 1.1 %copy-start = (bf16[1,2,64,1280]{3,2,1,0:T(8,128)(2,1)S(1)}, bf16[1,2,64,1280]{3,2,1,0:T(8,128)(2,1)}, u32[]{:S(2)}) copy-start(bf16[1,2,64,1280]{3,2,1,0:T(8,128)(2,1)} %get-tuple-element.8) | copy-start | bytes 983044

commit v2 on v1

--- a/solution.py
+++ b/solution.py
@@ -44,10 +44,11 @@
 
 
 def kernel(
-    sizes, features, q_ref, k_ref, v_ref, t_ref, gq_ref, gk_ref, kept_ref,
+    sizes, features, q_hbm, k_hbm, v_hbm, t_hbm, gq_hbm, gk_hbm, kept_hbm,
     oq_ref, ok_ref, ov_ref,
     kv, qn, bias, gx_out, gx_in, gy_out, gy_in, own, dq, acc, hx_out, hx_in,
     row_s, row_r, fr_s, fr_r, co_s, co_r, gx_s, gx_r, gy_s, gy_r, hx_s, hx_r,
+    q_ref, k_ref, v_ref, t_ref, gq_ref, gk_ref, kept_ref, load_s,
 ):
     frames, rows, heads = sizes
     chunks, _, _, _, width, wide = kv.shape
@@ -60,6 +61,17 @@
     has_f = [f_at > 0, f_at < frames - 1]
     has_r = [r_at > 0, r_at < rows - 1]
 
+    loads = [
+        pltpu.make_async_copy(src, dst, load_s.at[i])
+        for i, (src, dst) in enumerate(
+            (
+                (q_hbm, q_ref), (k_hbm, k_ref), (v_hbm, v_ref), (kept_hbm, kept_ref),
+                (gk_hbm, gk_ref.at[0]), (gq_hbm, gq_ref.at[0]), (t_hbm, t_ref),
+            )
+        )
+    ]
+    for load in loads:
+        load.start()
     barrier = pltpu.get_barrier_semaphore()
     pl.semaphore_signal(barrier, inc=1, device_id=head_id, device_id_type=MESH)
     for s in (0, 1):
@@ -113,8 +125,6 @@
     def lanes(c):
         return slice(c * wide, (c + 1) * wide)
 
-    for c in range(chunks):
-        kv[c, 1, 1, 1:3] = v_ref[0, :, :, lanes(c)]
     for s in (0, 1):
 
         @pl.when(jnp.logical_not(has_f[s]))
@@ -137,6 +147,8 @@
 
             lax.fori_loop(0, chunks, body, 0)
 
+    loads[0].wait()
+    loads[1].wait()
     square_q = jnp.zeros((tokens, 128), F32)
     square_k = jnp.zeros((tokens, 128), F32)
     for i in range(chunks * per):
@@ -149,6 +161,9 @@
         jnp.sum(square_q, -1, keepdims=True), jnp.sum(square_k, -1, keepdims=True)
     )
 
+    loads[2].wait()
+    for c in range(chunks):
+        kv[c, 1, 1, 1:3] = v_ref[0, :, :, lanes(c)]
     peers = 1
     for edge in (*has_f, *has_r):
         peers = peers + edge.astype(jnp.int32)
@@ -173,6 +188,7 @@
 
     lax.fori_loop(0, chunks, v_body, 0)
 
+    loads[3].wait()
     keys = 12 * width
     key = lax.broadcasted_iota(jnp.int32, (1, keys), 1)
     key_line = key // TC
@@ -184,7 +200,7 @@
             row = 2 * r_at + (g - 1)
             ok = jnp.logical_and(frame_ok, jnp.logical_and(row >= 0, row < 2 * rows))
             for tile in range(TILES):
-                one = kept_ref[jnp.clip(frame, 0, frames - 1), jnp.clip(row, 0, 2 * rows - 1), tile]
+                one = kept_ref[jnp.clip(frame, 0, frames - 1), tile, jnp.clip(row, 0, 2 * rows - 1)]
                 one = jnp.where(ok, one, 0)
                 kept_row = jnp.where(key_line == (d * 4 + g) * TILES + tile, one, kept_row)
     query = lax.broadcasted_iota(jnp.int32, (tokens, keys), 0)
@@ -197,6 +213,8 @@
     kept_full = jnp.broadcast_to(kept_row, (tokens, keys)) > 0
     bias[...] = jnp.where(near & (kept_full | same), 0.0, NEG)
 
+    for load in loads[4:]:
+        load.wait()
     hx_copy(0).wait()
     scale_q, scale_k = rows_to_columns(
         lax.rsqrt((hx_out[0] + hx_in[0]) / features + norm_eps)
@@ -384,7 +402,7 @@
     return pl.pallas_call(
         functools.partial(kernel, sizes, feat_dev * sizes[2]),
         out_shape=(out, out, out),
-        in_specs=[vmem] * 6 + [pl.BlockSpec(memory_space=pltpu.SMEM)],
+        in_specs=[pl.BlockSpec(memory_space=pltpu.HBM)] * 7,
         out_specs=(vmem, vmem, vmem),
         scratch_shapes=[
             pltpu.VMEM((chunks, 2, 3, 4, width, wide), BF16),
@@ -411,9 +429,14 @@
             dma((chunks, 2)),
             dma((2,)),
             dma((2,)),
+            *([pltpu.VMEM(q_pre.shape, BF16)] * 4),
+            pltpu.VMEM((1, feat_dev), F32),
+            pltpu.VMEM((1, feat_dev), F32),
+            pltpu.SMEM((kept.shape[0], TILES, kept.shape[1]), jnp.int32),
+            dma((7,)),
         ],
-        compiler_params=pltpu.CompilerParams(collective_id=0, has_side_effects=True),
-    )(q_pre, k_pre, values, target, gain_q[None], gain_k[None], kept)
+        compiler_params=pltpu.CompilerParams(vmem_limit_bytes=60 << 20, collective_id=0, has_side_effects=True),
+    )(q_pre, k_pre, values, target, gain_q, gain_k, kept.transpose(0, 2, 1))
 
 
 def solution(mesh):

time: 68.8 us -> 60.2 us (0.88)
  Pallas kernels: 60.8 us -> 55.8 us
  local copies, waits for them, and re-layouts: 7.04 us -> 3.58 us
    pallas_call x1, Pallas kernels: 60.8 us -> 55.8 us  [per_device(): pl.pallas_call(functools.partial(kernel, sizes, feat_dev * sizes[2]), out...]
    broadcast_in_dim x2 -> x0, local copies, waits for them, and re-layouts: 2.59 us -> none  [the longest x1 1.3 us: per_device(): gain_q[None]]
    unnamed x10 -> x7, local copies, waits for them, and re-layouts: 4.45 us -> 3.58 us
where the time goes in v2:
time: 60.2 us; the launch traced here: 60 us
  Pallas kernels  55.8 us (93%)
  local copies, waits for them, and re-layouts  3.58 us (6%)
  between operations  0.65 us (1%)
    pallas_call x1, Pallas kernels, per_device(): pl.pallas_call(functools.partial(kernel, sizes, feat_dev * sizes[2]), out...  55.8 us
    unnamed x7, local copies, waits for them, and re-layouts  3.58 us

profile of v2, /device:TPU:30, one launch (start us, length us, event | category | flops | bytes accessed | tf_op | source)
XLA Modules:
  0.0 60.0 jit_solution(14912274294762630837)
XLA Ops:
  0.6 55.8 %shard_map.94 = (bf16[1,2,64,1280]{3,2,1,0:T(8,128)(2,1)}, bf16[1,2,64,1280]{3,2,1,0:T(8,128)(2,1)}, bf16[1,2,64,1280]{3,2,1,0:T(8,128)(2,1)}) custom-call(bf16[1,2,64,1280]{3,2,1,0:T(8,128)(2,1)} %q_hbm.1, bf16[1,2,64,1280]{3,2,1,0:T(8,128)(2,1)} %k_hbm.1, bf16[1,2,64,1280]{3,2,1,0:T(8,128)(2,1)} %v_hbm.1, bf16[1,2,64,1280]{3,2,1,0:T(8,128)(2,1)} %t_hbm.1, ...), custom_call_target="tpu_custom_call" | custom-call | tf_op jit(solution)/shard_map/pallas_call | solution.py:402
  56.4 0.0 copy-start.1
  56.4 1.8 %copy.13 = bf16[1,2,64,1280]{3,2,1,0:T(8,128)(2,1)} copy(bf16[1,2,64,1280]{3,2,1,0:T(8,128)(2,1)} %get-tuple-element.6) | data formatting | bytes 655360
  58.2 0.0 copy-done.1
  58.2 0.0 copy-start
  58.2 0.7 %copy.14 = bf16[1,2,64,1280]{3,2,1,0:T(8,128)(2,1)} copy(bf16[1,2,64,1280]{3,2,1,0:T(8,128)(2,1)S(1)} %copy-done.1) | data formatting | bytes 655360
  58.9 0.4 copy-done
  59.3 0.7 %copy.15 = bf16[1,2,64,1280]{3,2,1,0:T(8,128)(2,1)} copy(bf16[1,2,64,1280]{3,2,1,0:T(8,128)(2,1)S(1)} %copy-done) | data formatting | bytes 655360
Async XLA Ops:
  56.4 1.8 %copy-start.1 = (bf16[1,2,64,1280]{3,2,1,0:T(8,128)(2,1)S(1)}, bf16[1,2,64,1280]{3,2,1,0:T(8,128)(2,1)}, u32[]{:S(2)}) copy-start(bf16[1,2,64,1280]{3,2,1,0:T(8,128)(2,1)} %get-tuple-element.7) | copy-start | bytes 983044
  58.2 1.1 %copy-start = (bf16[1,2,64,1280]{3,2,1,0:T(8,128)(2,1)S(1)}, bf16[1,2,64,1280]{3,2,1,0:T(8,128)(2,1)}, u32[]{:S(2)}) copy-start(bf16[1,2,64,1280]{3,2,1,0:T(8,128)(2,1)} %get-tuple-element.8) | copy-start | bytes 983044

commit v3 on v2

--- a/solution.py
+++ b/solution.py
@@ -49,6 +49,7 @@
     kv, qn, bias, gx_out, gx_in, gy_out, gy_in, own, dq, acc, hx_out, hx_in,
     row_s, row_r, fr_s, fr_r, co_s, co_r, gx_s, gx_r, gy_s, gy_r, hx_s, hx_r,
     q_ref, k_ref, v_ref, t_ref, gq_ref, gk_ref, kept_ref, load_s,
+    w_out, w_in, wx_out, wx_in, wy_out, wy_in, w_s, w_r, wx_s, wx_r, wy_s, wy_r,
 ):
     frames, rows, heads = sizes
     chunks, _, _, _, width, wide = kv.shape
@@ -119,6 +120,17 @@
         return remote(gy_out.at[c, s], gy_in.at[c, s if mine else 1 - s],
                       gy_s.at[c, s], gy_r.at[c, s if mine else 1 - s], row_id[s])
 
+    def w_copy():
+        return remote(w_out, w_in, w_s.at[0], w_r.at[0], head_id)
+
+    def wx_copy(s, mine):
+        return remote(wx_out.at[s], wx_in.at[s if mine else 1 - s],
+                      wx_s.at[s], wx_r.at[s if mine else 1 - s], frame_id[s])
+
+    def wy_copy(s, mine):
+        return remote(wy_out.at[s], wy_in.at[s if mine else 1 - s],
+                      wy_s.at[s], wy_r.at[s if mine else 1 - s], row_id[s])
+
     def hx_copy(i):
         return remote(hx_out.at[i], hx_in.at[i], hx_s.at[i], hx_r.at[i], head_id)
 
@@ -129,6 +141,8 @@
 
         @pl.when(jnp.logical_not(has_f[s]))
         def _():
+            wx_in[s] = jnp.zeros((1, 4 * width), F32)
+
             def body(c, carry):
                 kv[c, :, 2 * s] = jnp.zeros((2, 4, width, wide), BF16)
                 gx_in[c, s] = jnp.zeros((2, 4, width, wide), BF16)
@@ -138,6 +152,8 @@
 
         @pl.when(jnp.logical_not(has_r[s]))
         def _():
+            wy_in[s] = jnp.zeros((1, 2 * width), F32)
+
             def body(c, carry):
                 for a in (0, 1):
                     for d in range(3):
@@ -248,6 +264,7 @@
         lax.fori_loop(0, chunks, relay, 0)
 
     acc[...] = jnp.zeros_like(acc)
+    w_out[...] = jnp.zeros_like(w_out)
 
     def finish_x(c):
         for s in (0, 1):
@@ -290,7 +307,8 @@
             query_h = qn[c, :, part]
             key_h = kv[c, 0, :, :, :, part].reshape(keys, HD)
             value_h = kv[c, 1, :, :, :, part].reshape(keys, HD)
-            scores = dot(query_h, key_h, COLS_T) * (SCORE_SCALE * LOG2E) + bias[...]
+            inner = dot(query_h, key_h, COLS_T)
+            scores = inner * (SCORE_SCALE * LOG2E) + bias[...]
             expo = jnp.exp2(scores - jnp.max(scores, -1, keepdims=True))
             prob = expo * (1.0 / jnp.sum(expo, -1, keepdims=True))
             prob_b = prob.astype(BF16)
@@ -300,10 +318,11 @@
             delta = jnp.sum(d_out.astype(F32) * attended, -1, keepdims=True)
             prob_grad = dot(d_out, value_h, COLS_T)
             score_grad = (prob * ((prob_grad - delta) * SCORE_SCALE)).astype(BF16)
+            w_out[...] += jnp.sum(score_grad.astype(F32) * inner, 0, keepdims=True)
             dq_h = dot(score_grad, key_h, PLAIN)
             gated = dq_h * gq_ref[:, at]
             dq[c, :, part] = gated
-            acc[0] += gated * q_ref[0, :, :, at].reshape(tokens, HD).astype(F32)
+            acc[...] += gated * q_ref[0, :, :, at].reshape(tokens, HD).astype(F32)
             for a, grad in (
                 (0, dot(score_grad, query_h, ROWS_T)),
                 (1, dot(prob_b, d_out, ROWS_T)),
@@ -326,45 +345,88 @@
 
     lax.fori_loop(0, chunks, compute, 0)
 
-    def last_x(c, carry):
-        finish_x(c)
-        return carry
-
-    lax.fori_loop(max(chunks - 2, 0), chunks, last_x, 0)
-
-    def finish_y(c, carry):
-        at = pl.ds(pl.multiple_of(c * wide, HD), wide)
-        for s in (0, 1):
-
-            @pl.when(has_r[s])
-            def _():
-                gy_copy(c, s, True).wait_recv()
-
-        ov_ref[0, :, :, at] = (own[c, 1, 1:3] + gy_in[c, :, 1].astype(F32)).astype(BF16)
-        gated = (own[c, 0, 1:3] + gy_in[c, :, 0].astype(F32)).reshape(tokens, wide) * gk_ref[:, at]
-        own[c, 0, 1:3] = gated.reshape(2, width, wide)
-        product = gated * k_ref[0, :, :, at].reshape(tokens, wide).astype(F32)
-        for j in range(per):
-            acc[1] += product[:, j * HD : (j + 1) * HD]
-        return carry
-
-    lax.fori_loop(0, chunks, finish_y, 0)
-
-    hx_out[1] = columns_to_rows(
-        jnp.sum(acc[0], -1, keepdims=True), jnp.sum(acc[1], -1, keepdims=True)
-    )
+    sum_q = jnp.sum(acc[...], -1, keepdims=True)
+    hx_out[1] = columns_to_rows(sum_q, sum_q)
+    w_copy().start()
     hx_copy(1).start()
+    w_copy().wait()
+    both = w_out[...] + w_in[...]
+    for s in (0, 1):
+        wx_out[s] = both[:, 8 * s * width : (8 * s + 4) * width]
+
+        @pl.when(has_f[s])
+        def _():
+            wx_copy(s, False).start()
+
     hx_copy(1).wait()
-    sum_q, sum_k = rows_to_columns((hx_out[1] + hx_in[1]) / features)
+    sum_q, _ = rows_to_columns((hx_out[1] + hx_in[1]) / features)
     back_q = scale_q * scale_q * scale_q * sum_q
-    back_k = scale_k * scale_k * scale_k * sum_k
     for c in range(chunks):
         q_float = q_ref[0, :, :, lanes(c)].reshape(tokens, wide).astype(F32)
         grad_q = scale_q * dq[c] - q_float * back_q
         oq_ref[0, :, :, lanes(c)] = grad_q.astype(BF16).reshape(2, width, wide)
+
+    def last_x(c, carry):
+        finish_x(c)
+        return carry
+
+    lax.fori_loop(max(chunks - 2, 0), chunks, last_x, 0)
+
+    for s in (0, 1):
+
+        @pl.when(has_f[s])
+        def _():
+            wx_copy(s, True).wait_recv()
+
+    mine = both[:, 4 * width : 8 * width] + wx_in[0] + wx_in[1]
+    halves = [mine[:, 0 : 2 * width], mine[:, 2 * width : 4 * width]]
+    for s in (0, 1):
+        wy_out[s] = halves[s]
+
+        @pl.when(has_r[s])
+        def _():
+            wy_copy(s, False).start()
+
+    def finish_y(c, carry):
+        at = pl.ds(pl.multiple_of(c * wide, HD), wide)
+        for s in (0, 1):
+
+            @pl.when(has_r[s])
+            def _():
+                gy_copy(c, s, True).wait_recv()
+
+        ov_ref[0, :, :, at] = (own[c, 1, 1:3] + gy_in[c, :, 1].astype(F32)).astype(BF16)
+        gated = (own[c, 0, 1:3] + gy_in[c, :, 0].astype(F32)).reshape(tokens, wide) * gk_ref[:, at]
+        own[c, 0, 1:3] = (gated * scale_k).reshape(2, width, wide)
+        return carry
+
+    lax.fori_loop(0, chunks, finish_y, 0)
+
+    for s in (0, 1):
+
+        @pl.when(has_r[s])
+        def _():
+            wy_copy(s, True).wait_recv()
+
+    first, second = (
+        jnp.broadcast_to(halves[s] + wy_in[s], (128, 128)).T for s in (0, 1)
+    )
+    sum_k = jnp.concatenate([first[width:], second[:width]], axis=0)[:, 0:1]
+    back_k = scale_k * scale_k * sum_k / features
+    for c in range(chunks):
         k_float = k_ref[0, :, :, lanes(c)].reshape(tokens, wide).astype(F32)
-        grad_k = scale_k * own[c, 0, 1:3].reshape(tokens, wide) - k_float * back_k
+        grad_k = own[c, 0, 1:3].reshape(tokens, wide) - k_float * back_k
         ok_ref[0, :, :, lanes(c)] = grad_k.astype(BF16).reshape(2, width, wide)
+
+    for s in (0, 1):
+
+        @pl.when(has_f[s])
+        def _():
+            wx_copy(s, False).wait_send()
+
+        @pl.when(has_r[s])
+        def _():
+            wy_copy(s, False).wait_send()
 
     def drain(c, carry):
         for s in (0, 1):
@@ -414,7 +476,7 @@
             pltpu.VMEM((chunks, 2, 2, width, wide), BF16),
             pltpu.VMEM((chunks, 2, 4, width, wide), F32),
             pltpu.VMEM((chunks, 2 * width, wide), F32),
-            pltpu.VMEM((2, 2 * width, HD), F32),
+            pltpu.VMEM((2 * width, HD), F32),
             pltpu.VMEM((2, 8, 128), F32),
             pltpu.VMEM((2, 8, 128), F32),
             dma((chunks, 2, 2)),
@@ -434,6 +496,12 @@
             pltpu.VMEM((1, feat_dev), F32),
             pltpu.SMEM((kept.shape[0], TILES, kept.shape[1]), jnp.int32),
             dma((7,)),
+            pltpu.VMEM((1, 12 * width), F32),
+            pltpu.VMEM((1, 12 * width), F32),
+            *([pltpu.VMEM((2, 1, 4 * width), F32)] * 2),
+            *([pltpu.VMEM((2, 1, 2 * width), F32)] * 2),
+            *([dma((1,))] * 2),
+            *([dma((2,))] * 4),
         ],
         compiler_params=pltpu.CompilerParams(vmem_limit_bytes=60 << 20, collective_id=0, has_side_effects=True),
     )(q_pre, k_pre, values, target, gain_q, gain_k, kept.transpose(0, 2, 1))

time: 60.2 us -> 56.2 us (0.934)
  the two profiles are of different devices: /device:TPU:30 before, /device:TPU:27 now
where the time goes in v3:
time: 56.2 us; the launch traced here: 56 us
  Pallas kernels  51.8 us (92%)
  local copies, waits for them, and re-layouts  3.58 us (6%)
  between operations  0.65 us (1%)
    pallas_call x1, Pallas kernels, per_device(): pl.pallas_call(functools.partial(kernel, sizes, feat_dev * sizes[2]), out...  51.8 us
    unnamed x7, local copies, waits for them, and re-layouts  3.58 us

profile of v3, /device:TPU:27, one launch (start us, length us, event | category | flops | bytes accessed | tf_op | source)
XLA Modules:
  0.0 56.0 jit_solution(9615685248337001590)
XLA Ops:
  0.6 51.8 %shard_map.94 = (bf16[1,2,64,1280]{3,2,1,0:T(8,128)(2,1)}, bf16[1,2,64,1280]{3,2,1,0:T(8,128)(2,1)}, bf16[1,2,64,1280]{3,2,1,0:T(8,128)(2,1)}) custom-call(bf16[1,2,64,1280]{3,2,1,0:T(8,128)(2,1)} %q_hbm.1, bf16[1,2,64,1280]{3,2,1,0:T(8,128)(2,1)} %k_hbm.1, bf16[1,2,64,1280]{3,2,1,0:T(8,128)(2,1)} %v_hbm.1, bf16[1,2,64,1280]{3,2,1,0:T(8,128)(2,1)} %t_hbm.1, ...), custom_call_target="tpu_custom_call" | custom-call | tf_op jit(solution)/shard_map/pallas_call | solution.py:464
  52.5 0.0 copy-start.1
  52.5 1.8 %copy.13 = bf16[1,2,64,1280]{3,2,1,0:T(8,128)(2,1)} copy(bf16[1,2,64,1280]{3,2,1,0:T(8,128)(2,1)} %get-tuple-element.6) | data formatting | bytes 655360
  54.2 0.0 copy-done.1
  54.2 0.0 copy-start
  54.2 0.7 %copy.14 = bf16[1,2,64,1280]{3,2,1,0:T(8,128)(2,1)} copy(bf16[1,2,64,1280]{3,2,1,0:T(8,128)(2,1)S(1)} %copy-done.1) | data formatting | bytes 655360
  55.0 0.4 copy-done
  55.3 0.7 %copy.15 = bf16[1,2,64,1280]{3,2,1,0:T(8,128)(2,1)} copy(bf16[1,2,64,1280]{3,2,1,0:T(8,128)(2,1)S(1)} %copy-done) | data formatting | bytes 655360
Async XLA Ops:
  52.5 1.8 %copy-start.1 = (bf16[1,2,64,1280]{3,2,1,0:T(8,128)(2,1)S(1)}, bf16[1,2,64,1280]{3,2,1,0:T(8,128)(2,1)}, u32[]{:S(2)}) copy-start(bf16[1,2,64,1280]{3,2,1,0:T(8,128)(2,1)} %get-tuple-element.7) | copy-start | bytes 983044
  54.2 1.1 %copy-start = (bf16[1,2,64,1280]{3,2,1,0:T(8,128)(2,1)S(1)}, bf16[1,2,64,1280]{3,2,1,0:T(8,128)(2,1)}, u32[]{:S(2)}) copy-start(bf16[1,2,64,1280]{3,2,1,0:T(8,128)(2,1)} %get-tuple-element.8) | copy-start | bytes 983044

commit v4 on v3

--- a/solution.py
+++ b/solution.py
@@ -112,6 +112,10 @@
         return remote(kv.at[c, a, 1, 3 * t], kv.at[c, a, 2 * s, 3 * t],
                       co_s.at[c, a, s, t], co_r.at[c, a, s, t], frame_id[s])
 
+    def corner_row_out(c, a, s, t):
+        return remote(kv.at[c, a, 2 * s, 1 + t], kv.at[c, a, 2 * s, 3 - 3 * t],
+                      co_s.at[c, a, s, t], co_r.at[c, a, s, 1 - t], row_id[t])
+
     def gx_copy(c, s, mine):
         return remote(gx_out.at[c, s], gx_in.at[c, s if mine else 1 - s],
                       gx_s.at[c, s], gx_r.at[c, s if mine else 1 - s], frame_id[s])
@@ -203,6 +207,37 @@
         return carry
 
     lax.fori_loop(0, chunks, v_body, 0)
+
+    def relay(a, c, carry):
+        @pl.when(c % 2 == 0)
+        def _():
+            for t in (0, 1):
+
+                @pl.when(has_r[t])
+                def _():
+                    row_in(c, a, t).wait_recv()
+
+                for s in (0, 1):
+
+                    @pl.when(jnp.logical_and(has_r[t], has_f[s]))
+                    def _():
+                        corner_out(c, a, s, t).start()
+
+        @pl.when(c % 2 == 1)
+        def _():
+            for s in (0, 1):
+
+                @pl.when(has_f[s])
+                def _():
+                    frame_in(c, a, s).wait_recv()
+
+                for t in (0, 1):
+
+                    @pl.when(jnp.logical_and(has_r[t], has_f[s]))
+                    def _():
+                        corner_row_out(c, a, s, t).start()
+
+        return carry
 
     loads[3].wait()
     keys = 12 * width
@@ -229,6 +264,7 @@
     kept_full = jnp.broadcast_to(kept_row, (tokens, keys)) > 0
     bias[...] = jnp.where(near & (kept_full | same), 0.0, NEG)
 
+    lax.fori_loop(0, chunks, functools.partial(relay, 1), 0)
     for load in loads[4:]:
         load.wait()
     hx_copy(0).wait()
@@ -244,24 +280,7 @@
         q_norm = q_ref[0, :, :, lanes(c)].reshape(tokens, wide).astype(F32) * scale_q
         qn[c] = (q_norm * gq_ref[:, lanes(c)]).astype(BF16)
 
-    for a in (1, 0):
-
-        def relay(c, carry, a=a):
-            for t in (0, 1):
-
-                @pl.when(has_r[t])
-                def _():
-                    row_in(c, a, t).wait_recv()
-
-                for s in (0, 1):
-
-                    @pl.when(jnp.logical_and(has_r[t], has_f[s]))
-                    def _():
-                        corner_out(c, a, s, t).start()
-
-            return carry
-
-        lax.fori_loop(0, chunks, relay, 0)
+    lax.fori_loop(0, chunks, functools.partial(relay, 0), 0)
 
     acc[...] = jnp.zeros_like(acc)
     w_out[...] = jnp.zeros_like(w_out)
@@ -289,10 +308,15 @@
     def compute(c, carry):
         for s in (0, 1):
 
-            @pl.when(has_f[s])
+            @pl.when(jnp.logical_and(has_f[s], c % 2 == 0))
             def _():
                 for a in (0, 1):
                     frame_in(c, a, s).wait_recv()
+
+            @pl.when(jnp.logical_and(has_r[s], c % 2 == 1))
+            def _():
+                for a in (0, 1):
+                    row_in(c, a, s).wait_recv()
 
             for t in (0, 1):
 
@@ -455,13 +479,31 @@
     lax.fori_loop(0, chunks, drain, 0)
 
 
+def hand_over(*refs):
+    sources, results, (held, in_s, out_s) = refs[:3], refs[3:6], refs[6:]
+    moves = [
+        (
+            pltpu.make_async_copy(sources[i], held.at[i], in_s.at[i]),
+            pltpu.make_async_copy(held.at[i], results[i], out_s.at[i]),
+        )
+        for i in range(3)
+    ]
+    for take, _ in moves:
+        take.start()
+    for take, give in moves:
+        take.wait()
+        give.start()
+    for _, give in moves:
+        give.wait()
+
+
 def per_device(sizes, per, q_pre, k_pre, values, target, gain_q, gain_k, kept):
     _, _, width, feat_dev = q_pre.shape
     chunks, wide = feat_dev // (per * HD), per * HD
     dma = pltpu.SemaphoreType.DMA
     vmem = pl.BlockSpec(memory_space=pltpu.VMEM)
     out = jax.ShapeDtypeStruct(q_pre.shape, BF16)
-    return pl.pallas_call(
+    grads = pl.pallas_call(
         functools.partial(kernel, sizes, feat_dev * sizes[2]),
         out_shape=(out, out, out),
         in_specs=[pl.BlockSpec(memory_space=pltpu.HBM)] * 7,
@@ -505,6 +547,15 @@
         ],
         compiler_params=pltpu.CompilerParams(vmem_limit_bytes=60 << 20, collective_id=0, has_side_effects=True),
     )(q_pre, k_pre, values, target, gain_q, gain_k, kept.transpose(0, 2, 1))
+    hbm = pl.BlockSpec(memory_space=pltpu.HBM)
+    return pl.pallas_call(
+        hand_over,
+        out_shape=(out, out, out),
+        in_specs=[hbm] * 3,
+        out_specs=(hbm, hbm, hbm),
+        scratch_shapes=[pltpu.VMEM((3, *q_pre.shape), BF16), dma((3,)), dma((3,))],
+        compiler_params=pltpu.CompilerParams(vmem_limit_bytes=60 << 20),
+    )(*grads)
 
 
 def solution(mesh):

time: 56.2 us -> 53.2 us (0.947)
  the two profiles are of different devices: /device:TPU:27 before, /device:TPU:68 now
where the time goes in v4:
time: 53.2 us; the launch traced here: 53.1 us
  Pallas kernels  52.4 us (98%)
  between operations  0.64 us (1%)
    pallas_call x1, Pallas kernels, per_device(): pl.pallas_call(functools.partial(kernel, sizes, feat_dev * sizes[2]), out...  50.5 us
    pallas_call x1, Pallas kernels, per_device(): pl.pallas_call(hand_over, out_shape=(out, out, out), in_specs=[hbm] * 3,...  1.96 us

profile of v4, /device:TPU:68, one launch (start us, length us, event | category | flops | bytes accessed | tf_op | source)
XLA Modules:
  0.0 53.1 jit_solution(15274487164516642818)
XLA Ops:
  0.6 50.5 %shard_map.94 = (bf16[1,2,64,1280]{3,2,1,0:T(8,128)(2,1)}, bf16[1,2,64,1280]{3,2,1,0:T(8,128)(2,1)}, bf16[1,2,64,1280]{3,2,1,0:T(8,128)(2,1)}) custom-call(bf16[1,2,64,1280]{3,2,1,0:T(8,128)(2,1)} %q_hbm.1, bf16[1,2,64,1280]{3,2,1,0:T(8,128)(2,1)} %k_hbm.1, bf16[1,2,64,1280]{3,2,1,0:T(8,128)(2,1)} %v_hbm.1, bf16[1,2,64,1280]{3,2,1,0:T(8,128)(2,1)} %t_hbm.1, ...), custom_call_target="tpu_custom_call" | custom-call | tf_op jit(solution)/shard_map/pallas_call | solution.py:506
  51.1 2.0 %shard_map.95 = (bf16[1,2,64,1280]{3,2,1,0:T(8,128)(2,1)}, bf16[1,2,64,1280]{3,2,1,0:T(8,128)(2,1)}, bf16[1,2,64,1280]{3,2,1,0:T(8,128)(2,1)}) custom-call(bf16[1,2,64,1280]{3,2,1,0:T(8,128)(2,1)} %get-tuple-element.6.refs_0_, bf16[1,2,64,1280]{3,2,1,0:T(8,128)(2,1)} %get-tuple-element.7.refs_1_, bf16[1,2,64,1280]{3,2,1,0:T(8,128)(2,1)} %get-tuple-element.8.refs_2_), custom_call_target="tpu_custom_call" | custom-call | tf_op jit(solution)/shard_map/pallas_call | solution.py:551

commit v5 on v4

--- a/solution.py
+++ b/solution.py
@@ -50,6 +50,7 @@
     row_s, row_r, fr_s, fr_r, co_s, co_r, gx_s, gx_r, gy_s, gy_r, hx_s, hx_r,
     q_ref, k_ref, v_ref, t_ref, gq_ref, gk_ref, kept_ref, load_s,
     w_out, w_in, wx_out, wx_in, wy_out, wy_in, w_s, w_r, wx_s, wx_r, wy_s, wy_r,
+    gc_in, gc_s, gc_r,
 ):
     frames, rows, heads = sizes
     chunks, _, _, _, width, wide = kv.shape
@@ -120,6 +121,14 @@
         return remote(gx_out.at[c, s], gx_in.at[c, s if mine else 1 - s],
                       gx_s.at[c, s], gx_r.at[c, s if mine else 1 - s], frame_id[s])
 
+    def gx_half(c, s, mine):
+        return remote(gx_out.at[c, s, :, pl.ds(1, 2)], gx_in.at[c, s if mine else 1 - s, :, pl.ds(1, 2)],
+                      gx_s.at[c, s], gx_r.at[c, s if mine else 1 - s], frame_id[s])
+
+    def gc_copy(c, t, s, mine):
+        return remote(gx_out.at[c, s, :, 3 * t], gc_in.at[c, t if mine else 1 - t, s],
+                      gc_s.at[c, t, s], gc_r.at[c, t if mine else 1 - t, s], row_id[t])
+
     def gy_copy(c, s, mine):
         return remote(gy_out.at[c, s], gy_in.at[c, s if mine else 1 - s],
                       gy_s.at[c, s], gy_r.at[c, s if mine else 1 - s], row_id[s])
@@ -163,6 +172,7 @@
                     for d in range(3):
                         kv[c, a, d, 3 * s] = jnp.zeros((width, wide), BF16)
                 gy_in[c, s] = jnp.zeros((2, width, wide), BF16)
+                gc_in[c, s] = jnp.zeros((2, 2, width, wide), BF16)
                 return carry
 
             lax.fori_loop(0, chunks, body, 0)
@@ -304,6 +314,40 @@
             @pl.when(has_r[s])
             def _():
                 gy_copy(c, s, False).start()
+
+    def finish_rows(c):
+        for t in (0, 1):
+
+            @pl.when(has_r[t])
+            def _():
+                gy_copy(c, t, True).wait_recv()
+
+            for s in (0, 1):
+
+                @pl.when(jnp.logical_and(has_r[t], has_f[s]))
+                def _():
+                    gc_copy(c, t, s, True).wait_recv()
+
+        for a in (0, 1):
+            for t in (0, 1):
+                own[c, a, 1 + t] += gy_in[c, t, a].astype(F32)
+                for s in (0, 1):
+                    total = gx_out[c, s, a, 1 + t].astype(F32) + gc_in[c, t, s, a].astype(F32)
+                    gx_out[c, s, a, 1 + t] = total.astype(BF16)
+        for s in (0, 1):
+
+            @pl.when(has_f[s])
+            def _():
+                gx_half(c, s, False).start()
+
+    def finish_first(c):
+        @pl.when(c % 2 == 0)
+        def _():
+            finish_x(c)
+
+        @pl.when(c % 2 == 1)
+        def _():
+            finish_rows(c)
 
     def compute(c, carry):
         for s in (0, 1):
@@ -353,17 +397,29 @@
             ):
                 grad = grad.reshape(3, 4, width, HD)
                 own[c, a, :, :, part] = grad[1]
+                for t in (0, 1):
+                    gy_out[c, t, a, :, part] = grad[1, 3 * t].astype(BF16)
                 for s in (0, 1):
                     gx_out[c, s, a, :, :, part] = grad[2 * s].astype(BF16)
         for s in (0, 1):
 
-            @pl.when(has_f[s])
+            @pl.when(jnp.logical_and(has_f[s], c % 2 == 0))
             def _():
                 gx_copy(c, s, False).start()
 
+            @pl.when(jnp.logical_and(has_r[s], c % 2 == 1))
+            def _():
+                gy_copy(c, s, False).start()
+
+            for t in (0, 1):
+
+                @pl.when(jnp.logical_and(jnp.logical_and(has_r[t], has_f[s]), c % 2 == 1))
+                def _():
+                    gc_copy(c, t, s, False).start()
+
         @pl.when(c >= 2)
         def _():
-            finish_x(c - 2)
+            finish_first(c - 2)
 
         return carry
 
@@ -391,7 +447,7 @@
         oq_ref[0, :, :, lanes(c)] = grad_q.astype(BF16).reshape(2, width, wide)
 
     def last_x(c, carry):
-        finish_x(c)
+        finish_first(c)
         return carry
 
     lax.fori_loop(max(chunks - 2, 0), chunks, last_x, 0)
@@ -411,20 +467,41 @@
         def _():
             wy_copy(s, False).start()
 
-    def finish_y(c, carry):
-        at = pl.ds(pl.multiple_of(c * wide, HD), wide)
-        for s in (0, 1):
-
-            @pl.when(has_r[s])
-            def _():
-                gy_copy(c, s, True).wait_recv()
-
-        ov_ref[0, :, :, at] = (own[c, 1, 1:3] + gy_in[c, :, 1].astype(F32)).astype(BF16)
-        gated = (own[c, 0, 1:3] + gy_in[c, :, 0].astype(F32)).reshape(tokens, wide) * gk_ref[:, at]
-        own[c, 0, 1:3] = (gated * scale_k).reshape(2, width, wide)
+    def finish_last(c, carry):
+        def put(a, total):
+            at = pl.ds(pl.multiple_of(c * wide, HD), wide)
+            if a == 1:
+                ov_ref[0, :, :, at] = total.astype(BF16)
+            else:
+                gated = total.reshape(tokens, wide) * gk_ref[:, at]
+                own[c, 0, 1:3] = (gated * scale_k).reshape(2, width, wide)
+
+        @pl.when(c % 2 == 0)
+        def _():
+            for s in (0, 1):
+
+                @pl.when(has_r[s])
+                def _():
+                    gy_copy(c, s, True).wait_recv()
+
+            for a in (0, 1):
+                put(a, own[c, a, 1:3] + gy_in[c, :, a].astype(F32))
+
+        @pl.when(c % 2 == 1)
+        def _():
+            for s in (0, 1):
+
+                @pl.when(has_f[s])
+                def _():
+                    gx_half(c, s, True).wait_recv()
+
+            for a in (0, 1):
+                moved = gx_in[c, 0, a, 1:3].astype(F32) + gx_in[c, 1, a, 1:3].astype(F32)
+                put(a, own[c, a, 1:3] + moved)
+
         return carry
 
-    lax.fori_loop(0, chunks, finish_y, 0)
+    lax.fori_loop(0, chunks, finish_last, 0)
 
     for s in (0, 1):
 
@@ -465,7 +542,14 @@
             def _():
                 for a in (0, 1):
                     frame_out(c, a, s).wait_send()
+
+            @pl.when(jnp.logical_and(has_f[s], c % 2 == 0))
+            def _():
                 gx_copy(c, s, False).wait_send()
+
+            @pl.when(jnp.logical_and(has_f[s], c % 2 == 1))
+            def _():
+                gx_half(c, s, False).wait_send()
 
             for t in (0, 1):
 
@@ -473,6 +557,10 @@
                 def _():
                     for a in (0, 1):
                         corner_out(c, a, s, t).wait_send()
+
+                @pl.when(jnp.logical_and(jnp.logical_and(has_r[t], has_f[s]), c % 2 == 1))
+                def _():
+                    gc_copy(c, t, s, False).wait_send()
 
         return carry
 
@@ -544,6 +632,8 @@
             *([pltpu.VMEM((2, 1, 2 * width), F32)] * 2),
             *([dma((1,))] * 2),
             *([dma((2,))] * 4),
+            pltpu.VMEM((chunks, 2, 2, 2, width, wide), BF16),
+            *([dma((chunks, 2, 2))] * 2),
         ],
         compiler_params=pltpu.CompilerParams(vmem_limit_bytes=60 << 20, collective_id=0, has_side_effects=True),
     )(q_pre, k_pre, values, target, gain_q, gain_k, kept.transpose(0, 2, 1))

time: 53.2 us -> 56.3 us (1.058)
  the two profiles are of different devices: /device:TPU:68 before, /device:TPU:3 now
where the time goes in v5:
time: 56.3 us; the launch traced here: 56.2 us
  Pallas kernels  55.5 us (99%)
  between operations  0.64 us (1%)
    pallas_call x1, Pallas kernels, per_device(): pl.pallas_call(functools.partial(kernel, sizes, feat_dev * sizes[2]), out...  53.6 us
    pallas_call x1, Pallas kernels, per_device(): pl.pallas_call(hand_over, out_shape=(out, out, out), in_specs=[hbm] * 3,...  1.96 us

profile of v5, /device:TPU:3, one launch (start us, length us, event | category | flops | bytes accessed | tf_op | source)
XLA Modules:
  0.0 56.2 jit_solution(4658374397327413044)
XLA Ops:
  0.6 53.6 %shard_map.94 = (bf16[1,2,64,1280]{3,2,1,0:T(8,128)(2,1)}, bf16[1,2,64,1280]{3,2,1,0:T(8,128)(2,1)}, bf16[1,2,64,1280]{3,2,1,0:T(8,128)(2,1)}) custom-call(bf16[1,2,64,1280]{3,2,1,0:T(8,128)(2,1)} %q_hbm.1, bf16[1,2,64,1280]{3,2,1,0:T(8,128)(2,1)} %k_hbm.1, bf16[1,2,64,1280]{3,2,1,0:T(8,128)(2,1)} %v_hbm.1, bf16[1,2,64,1280]{3,2,1,0:T(8,128)(2,1)} %t_hbm.1, ...), custom_call_target="tpu_custom_call" | custom-call | tf_op jit(solution)/shard_map/pallas_call | solution.py:594
  54.2 2.0 %shard_map.95 = (bf16[1,2,64,1280]{3,2,1,0:T(8,128)(2,1)}, bf16[1,2,64,1280]{3,2,1,0:T(8,128)(2,1)}, bf16[1,2,64,1280]{3,2,1,0:T(8,128)(2,1)}) custom-call(bf16[1,2,64,1280]{3,2,1,0:T(8,128)(2,1)} %get-tuple-element.6.refs_0_, bf16[1,2,64,1280]{3,2,1,0:T(8,128)(2,1)} %get-tuple-element.7.refs_1_, bf16[1,2,64,1280]{3,2,1,0:T(8,128)(2,1)} %get-tuple-element.8.refs_2_), custom_call_target="tpu_custom_call" | custom-call | tf_op jit(solution)/shard_map/pallas_call | solution.py:641

commit v6 on v4

--- a/solution.py
+++ b/solution.py
@@ -112,10 +112,6 @@
         return remote(kv.at[c, a, 1, 3 * t], kv.at[c, a, 2 * s, 3 * t],
                       co_s.at[c, a, s, t], co_r.at[c, a, s, t], frame_id[s])
 
-    def corner_row_out(c, a, s, t):
-        return remote(kv.at[c, a, 2 * s, 1 + t], kv.at[c, a, 2 * s, 3 - 3 * t],
-                      co_s.at[c, a, s, t], co_r.at[c, a, s, 1 - t], row_id[t])
-
     def gx_copy(c, s, mine):
         return remote(gx_out.at[c, s], gx_in.at[c, s if mine else 1 - s],
                       gx_s.at[c, s], gx_r.at[c, s if mine else 1 - s], frame_id[s])
@@ -209,33 +205,17 @@
     lax.fori_loop(0, chunks, v_body, 0)
 
     def relay(a, c, carry):
-        @pl.when(c % 2 == 0)
-        def _():
-            for t in (0, 1):
-
-                @pl.when(has_r[t])
+        for t in (0, 1):
+
+            @pl.when(has_r[t])
+            def _():
+                row_in(c, a, t).wait_recv()
+
+            for s in (0, 1):
+
+                @pl.when(jnp.logical_and(has_r[t], has_f[s]))
                 def _():
-                    row_in(c, a, t).wait_recv()
-
-                for s in (0, 1):
-
-                    @pl.when(jnp.logical_and(has_r[t], has_f[s]))
-                    def _():
-                        corner_out(c, a, s, t).start()
-
-        @pl.when(c % 2 == 1)
-        def _():
-            for s in (0, 1):
-
-                @pl.when(has_f[s])
-                def _():
-                    frame_in(c, a, s).wait_recv()
-
-                for t in (0, 1):
-
-                    @pl.when(jnp.logical_and(has_r[t], has_f[s]))
-                    def _():
-                        corner_row_out(c, a, s, t).start()
+                    corner_out(c, a, s, t).start()
 
         return carry
 
@@ -308,15 +288,10 @@
     def compute(c, carry):
         for s in (0, 1):
 
-            @pl.when(jnp.logical_and(has_f[s], c % 2 == 0))
+            @pl.when(has_f[s])
             def _():
                 for a in (0, 1):
                     frame_in(c, a, s).wait_recv()
-
-            @pl.when(jnp.logical_and(has_r[s], c % 2 == 1))
-            def _():
-                for a in (0, 1):
-                    row_in(c, a, s).wait_recv()
 
             for t in (0, 1):
 

time: 53.2 us -> 53 us (level)
  the two profiles are of different devices: /device:TPU:68 before, /device:TPU:67 now
where the time goes in v6:
time: 53 us; the launch traced here: 52.8 us
  Pallas kernels  52.2 us (98%)
  between operations  0.64 us (1%)
    pallas_call x1, Pallas kernels, per_device(): pl.pallas_call(functools.partial(kernel, sizes, feat_dev * sizes[2]), out...  50.2 us
    pallas_call x1, Pallas kernels, per_device(): pl.pallas_call(hand_over, out_shape=(out, out, out), in_specs=[hbm] * 3,...  1.96 us

profile of v6, /device:TPU:67, one launch (start us, length us, event | category | flops | bytes accessed | tf_op | source)
XLA Modules:
  0.0 52.8 jit_solution(3507363076365340799)
XLA Ops:
  0.6 50.2 %shard_map.94 = (bf16[1,2,64,1280]{3,2,1,0:T(8,128)(2,1)}, bf16[1,2,64,1280]{3,2,1,0:T(8,128)(2,1)}, bf16[1,2,64,1280]{3,2,1,0:T(8,128)(2,1)}) custom-call(bf16[1,2,64,1280]{3,2,1,0:T(8,128)(2,1)} %q_hbm.1, bf16[1,2,64,1280]{3,2,1,0:T(8,128)(2,1)} %k_hbm.1, bf16[1,2,64,1280]{3,2,1,0:T(8,128)(2,1)} %v_hbm.1, bf16[1,2,64,1280]{3,2,1,0:T(8,128)(2,1)} %t_hbm.1, ...), custom_call_target="tpu_custom_call" | custom-call | tf_op jit(solution)/shard_map/pallas_call | solution.py:481
  50.9 2.0 %shard_map.95 = (bf16[1,2,64,1280]{3,2,1,0:T(8,128)(2,1)}, bf16[1,2,64,1280]{3,2,1,0:T(8,128)(2,1)}, bf16[1,2,64,1280]{3,2,1,0:T(8,128)(2,1)}) custom-call(bf16[1,2,64,1280]{3,2,1,0:T(8,128)(2,1)} %get-tuple-element.6.refs_0_, bf16[1,2,64,1280]{3,2,1,0:T(8,128)(2,1)} %get-tuple-element.7.refs_1_, bf16[1,2,64,1280]{3,2,1,0:T(8,128)(2,1)} %get-tuple-element.8.refs_2_), custom_call_target="tpu_custom_call" | custom-call | tf_op jit(solution)/shard_map/pallas_call | solution.py:526
